TPU v7x, 32 devices: a whole 2x2x4 slice. The times are simulated.
32 devices in a mesh: grp: 4 (over y, x), rep: 8 (over z, core).
Axes of the slice: x: 2, y: 2, z: 4, core: 2. Of those that a mesh axis runs over, the one named last changes fastest.
Arguments:
- block_input: bfloat16 [32, 1024, 512], P(('grp', 'rep')), may hold values from -11 to 11
- cotangent: bfloat16 [32, 1024, 512], P(('grp', 'rep')), may hold values from -6 to 6
- encoder_states: bfloat16 [32, 512, 512], P(('grp', 'rep')), may hold values from -6 to 6
- segment_ids: int32 [32, 1024], P(('grp', 'rep')), may hold values from 0 to 5, as said below
- bucket_table: int32 [1024], replicated, may hold values from 0 to 31, as said below
- w_attn: float32 [6, 512, 384], P(None, 'grp'), may hold values from -0.125 to 0.125
- w_attn_out: float32 [2, 384, 512], P(None, None, 'grp'), may hold values from -1.75 to 1.75
- w_ff_in: float32 [2, 512, 1024], P(None, 'grp'), may hold values from -0.25 to 0.25
- w_ff_out: float32 [1024, 512], P(None, 'grp'), may hold values from -0.1875 to 0.1875
- norm_gains: float32 [3, 512], P(None, 'grp'), may hold values from 0.5 to 1.5
- rel_bias: float32 [32, 6], P('grp'), may hold values from -3 to 3
- mom_attn: float32 [6, 512, 384], P(None, 'grp'), may hold values from -128 to 128
- mom_attn_out: float32 [2, 384, 512], P(None, None, 'grp'), may hold values from -6 to 6
- mom_ff_in: float32 [2, 512, 1024], P(None, 'grp'), may hold values from -28 to 28
- mom_ff_out: float32 [1024, 512], P(None, 'grp'), may hold values from -28 to 28
- mom_gains: float32 [3, 512], P(None, 'grp'), may hold values from -256 to 256
- mom_bias: float32 [32, 6], P('grp'), may hold values from -256 to 256
- err_attn: float32 [8, 6, 512, 384], P('rep', None, 'grp'), may hold values from -1024 to 1024
- err_attn_out: float32 [8, 2, 384, 512], P('rep', None, None, 'grp'), may hold values from -48 to 48
- err_ff_in: float32 [8, 2, 512, 1024], P('rep', None, 'grp'), may hold values from -224 to 224
- err_ff_out: float32 [8, 1024, 512], P('rep', None, 'grp'), may hold values from -224 to 224
- q_start: float32 [11, 512, 8], P(None, 'grp'), may hold values from -6 to 6
Outputs:
- block_output: bfloat16 [32, 1024, 512], P(('grp', 'rep'))
- input_grad: float32 [32, 1024, 512], P(('grp', 'rep'))
- encoder_grad: float32 [32, 512, 512], P(('grp', 'rep'))
- branch_rms: float32 [4], replicated
- grad_attn: float32 [8, 6, 512, 384], P('rep', None, 'grp')
- grad_attn_out: float32 [8, 2, 384, 512], P('rep', None, None, 'grp')
- grad_ff_in: float32 [8, 2, 512, 1024], P('rep', None, 'grp')
- grad_ff_out: float32 [8, 1024, 512], P('rep', None, 'grp')
- grad_gains: float32 [8, 3, 512], P('rep', None, 'grp')
- grad_bias: float32 [8, 32, 6], P('rep', 'grp')
- new_err_attn: float32 [8, 6, 512, 384], P('rep', None, 'grp')
- new_err_attn_out: float32 [8, 2, 384, 512], P('rep', None, None, 'grp')
- new_err_ff_in: float32 [8, 2, 512, 1024], P('rep', None, 'grp')
- new_err_ff_out: float32 [8, 1024, 512], P('rep', None, 'grp')
- new_mom_attn: float32 [6, 512, 384], P(None, 'grp')
- new_mom_attn_out: float32 [2, 384, 512], P(None, None, 'grp')
- new_mom_ff_in: float32 [2, 512, 1024], P(None, 'grp')
- new_mom_ff_out: float32 [1024, 512], P(None, 'grp')
- new_mom_gains: float32 [3, 512], P(None, 'grp')
- new_mom_bias: float32 [32, 6], P('grp')
- update_attn: float32 [6, 512, 384], P(None, 'grp')
- update_attn_out: float32 [2, 384, 512], P(None, None, 'grp')
- update_ff_in: float32 [2, 512, 1024], P(None, 'grp')
- update_ff_out: float32 [1024, 512], P(None, 'grp')
- update_gains: float32 [3, 512], P(None, 'grp')
- update_bias: float32 [32, 6], P('grp')
- new_factors: float32 [11, 512, 8], P(None, 'grp')
Inputs may be any that keep to these rules, and one draw needn't show every extreme that they name: `segment_ids`: in each sequence the tokens before a tail of 1 to 768 positions carry document numbers that start at 1, never fall and end at the sequence's count of documents, which is 5 in every sequence; the tail carries 0. bucket_table[d] belongs to distance d: it equals d for d up to 16, never falls, and is 31 at the last distance.
All inputs are finite; a program needn't handle non-finite values.
Results may differ from a plain program's by a relative error of at most 0.025.
The roundings to bfloat16 on the way count: a program that leaves them out, or rounds other values in their place, can miss the bound.
Values may be sent and summed in bfloat16 or wider, within the bound.
No kernel may reach another device: no remote copies, remote signals or barrier semaphores. Data moves between devices by JAX's collectives and lax.ppermute only.
A program may use at most 320 MiB of HBM per device.

v0:
```python
import functools

import jax
import jax.numpy as jnp
from jax import lax
from jax.experimental import pallas as pl
from jax.experimental.pallas import tpu as pltpu
from jax.sharding import PartitionSpec as P

H = 6
DK = 64
PAIR = 2 * DK
ROWS = 256
SHARE = 128

epsilon = 1e-06
decay = 0.5
rates = (0.002, 0.5, 0.015, 0.015, 0.005, 0.05)
masked_score = -1e30
highest = lax.Precision.HIGHEST
NT = (((1,), (1,)), ((), ()))
NN = (((1,), (0,)), ((), ()))
TN = (((0,), (0,)), ((), ()))
f32 = jnp.float32
bf16 = jnp.bfloat16


def mm(left, right, dims=NN):
    return lax.dot_general(left, right, dims, preferred_element_type=f32)


def bias_kernel(length, bucket_ref, table_ref, out_ref):
    buckets = table_ref.shape[0]
    bucket = bucket_ref[...]
    match = lax.broadcasted_iota(jnp.int32, (buckets, length), 0) == bucket
    by_gap = mm(table_ref[...], match.astype(bf16), TN)
    tiles = length // ROWS
    wide = 2 * ROWS
    padded = jnp.concatenate(
        [jnp.full((H, ROWS), masked_score, f32), by_gap], axis=1
    )
    for head in range(H):
        for tile in range(tiles):
            first = length - ROWS * (tile + 1)
            line = padded[head : head + 1, first : first + wide]
            rows = jnp.concatenate(
                [line] + [pltpu.roll(line, step, 1) for step in range(1, 8)], axis=0
            )
            while rows.shape[0] < ROWS:
                rows = jnp.concatenate([rows, pltpu.roll(rows, rows.shape[0], 1)], axis=0)
            out_ref[head, ROWS * tile : ROWS * (tile + 1), :] = rows[:, ROWS:]


def bias_tiles(bucket_table, table_low):
    length = bucket_table.shape[0]
    return pl.pallas_call(
        functools.partial(bias_kernel, length),
        out_shape=jax.ShapeDtypeStruct((H, length, ROWS), f32),
        name="bias_tiles",
    )(bucket_table.reshape(1, length), table_low)


def lane_masks(rows):
    lane = lax.broadcasted_iota(jnp.int32, (rows, PAIR), 1)
    return (lane < DK, lane >= DK)


def turned(value):
    return value.astype(f32).T.astype(bf16)


def scores_of(q_ref, keys, bias_ref, qseg_ref, first, count, half, mask):
    query = q_ref[first : first + ROWS, :]
    query = jnp.where(mask, query, jnp.zeros_like(query))
    full = query
    if qseg_ref is not None:
        full = jnp.concatenate([query, qseg_ref[first : first + ROWS, :]], axis=1)
    scores = mm(keys[:count], full, NT)
    if bias_ref is not None:
        length = bias_ref.shape[1]
        scores = scores + bias_ref[half, length - count : length, :]
    return query, scores


def forward_kernel(causal, *refs):
    if causal:
        q_ref, k_ref, v_ref, bias_ref, kseg_ref, qseg_ref, out_ref, log_ref = refs
        keys = jnp.concatenate([k_ref[...], kseg_ref[...]], axis=1)
    else:
        q_ref, k_ref, v_ref, out_ref, log_ref = refs
        bias_ref = qseg_ref = None
        keys = k_ref[...]
    length = q_ref.shape[0]
    values = turned(v_ref[...])
    masks = lane_masks(ROWS)
    log_ref[...] = jnp.zeros_like(log_ref)
    for first in range(0, length, ROWS):
        count = first + ROWS if causal else keys.shape[0]
        mixed = []
        for half in range(2):
            unused, scores = scores_of(
                q_ref, keys, bias_ref, qseg_ref, first, count, half, masks[half]
            )
            top = jnp.max(scores, axis=0, keepdims=True)
            powers = jnp.exp(scores - top)
            total = jnp.sum(powers, axis=0, keepdims=True)
            probs = (powers * (1.0 / total)).astype(bf16)
            mixed.append(mm(values[DK * half : DK * (half + 1), :count], probs))
            log_ref[half : half + 1, first : first + ROWS] = top + jnp.log(total)
        out_ref[first : first + ROWS, :] = jnp.concatenate(mixed, axis=0).T.astype(bf16)


def squeezed(rows, index):
    return pl.BlockSpec((None, rows, PAIR), index)


def column(rows):
    return pl.BlockSpec((rows, PAIR), lambda p: (0, p))


def whole(shape):
    return pl.BlockSpec(shape, lambda p: (0,) * len(shape))


def log_spec(length):
    return pl.BlockSpec((None, 8, length), lambda p: (p, 0, 0))


def bias_spec(length):
    return pl.BlockSpec((2, length, ROWS), lambda p: (p, 0, 0))


def self_forward(heads, bias, kseg, qseg):
    length = heads.shape[1]
    pairs = H // 2
    return pl.pallas_call(
        functools.partial(forward_kernel, True),
        grid=(pairs,),
        in_specs=[
            squeezed(length, lambda p: (0, 0, p)),
            squeezed(length, lambda p: (1, 0, p)),
            squeezed(length, lambda p: (2, 0, p)),
            bias_spec(length),
            whole((length, PAIR)),
            whole((length, PAIR)),
        ],
        out_specs=[column(length), log_spec(length)],
        out_shape=[
            jax.ShapeDtypeStruct((length, H * DK), bf16),
            jax.ShapeDtypeStruct((pairs, 8, length), f32),
        ],
        name="self_forward",
    )(heads, heads, heads, bias, kseg, qseg)


def cross_forward(query, pairs_kv):
    length = query.shape[0]
    states = pairs_kv.shape[1]
    pairs = H // 2
    return pl.pallas_call(
        functools.partial(forward_kernel, False),
        grid=(pairs,),
        in_specs=[
            column(length),
            squeezed(states, lambda p: (0, 0, p)),
            squeezed(states, lambda p: (1, 0, p)),
        ],
        out_specs=[column(length), log_spec(length)],
        out_shape=[
            jax.ShapeDtypeStruct((length, H * DK), bf16),
            jax.ShapeDtypeStruct((pairs, 8, length), f32),
        ],
        name="cross_forward",
    )(query, pairs_kv, pairs_kv)


def backward_kernel(causal, *refs):
    if causal:
        (q_ref, k_ref, v_ref, grad_ref, log_ref, bias_ref, kseg_ref, qseg_ref, bucket_ref,
         out_ref, table_ref, key_sum, value_sum, tile_sum) = refs
        keys = jnp.concatenate([k_ref[...], kseg_ref[...]], axis=1)
        tile_sum[...] = jnp.zeros_like(tile_sum)
    else:
        q_ref, k_ref, v_ref, grad_ref, log_ref, dq_ref, pair_ref, key_sum, value_sum = refs
        bias_ref = qseg_ref = None
        keys = k_ref[...]
    length = q_ref.shape[0]
    states = keys.shape[0]
    turned_keys = turned(k_ref[...])
    masks = lane_masks(ROWS)
    key_sum[...] = jnp.zeros_like(key_sum)
    value_sum[...] = jnp.zeros_like(value_sum)
    for first in range(0, length, ROWS):
        count = first + ROWS if causal else states
        query_grads = []
        for half in range(2):
            query, scores = scores_of(
                q_ref, keys, bias_ref, qseg_ref, first, count, half, masks[half]
            )
            probs = jnp.exp(scores - log_ref[half : half + 1, first : first + ROWS])
            grad = grad_ref[first : first + ROWS, :]
            grad = jnp.where(masks[half], grad, jnp.zeros_like(grad))
            grad_probs = mm(v_ref[:count, :], grad, NT)
            dots = jnp.sum(grad_probs * probs, axis=0, keepdims=True)
            grad_scores = (probs * (grad_probs - dots)).astype(bf16)
            value_sum[:count, :] += mm(probs.astype(bf16), grad)
            key_sum[:count, :] += mm(grad_scores, query)
            query_grads.append(mm(turned_keys[DK * half : DK * (half + 1), :count], grad_scores))
            if causal:
                tile_sum[half, length - count : length, :] += grad_scores.astype(f32)
        joined = jnp.concatenate(query_grads, axis=0).T.astype(bf16)
        if causal:
            out_ref[0, first : first + ROWS, :] = joined
        else:
            dq_ref[first : first + ROWS, :] = joined
    if causal:
        out_ref[1] = key_sum[...].astype(bf16)
        out_ref[2] = value_sum[...].astype(bf16)
        by_gap = jnp.concatenate(
            [diagonal_sums(tile_sum, half) for half in range(2)]
            + [jnp.zeros((6, length), f32)],
            axis=0,
        )
        match = lax.broadcasted_iota(jnp.int32, (SHARE, length), 0) == bucket_ref[...]
        table_ref[...] = lax.dot_general(
            by_gap, match.astype(f32), NT,
            precision=lax.Precision.HIGHEST, preferred_element_type=f32,
        )
    else:
        pair_ref[0] = key_sum[...].astype(bf16)
        pair_ref[1] = value_sum[...].astype(bf16)


def diagonal_sums(tile_sum, half):
    length = tile_sum.shape[1]
    wide = 2 * ROWS
    pieces = []
    carried = None
    for tile in range(length // ROWS):
        rows = tile_sum[half, ROWS * tile : ROWS * (tile + 1), :]
        rows = jnp.concatenate([rows, jnp.zeros_like(rows)], axis=1)
        while rows.shape[0] > 1:
            middle = rows.shape[0] // 2
            rows = rows[:middle] + pltpu.roll(rows[middle:], wide - middle, 1)
        low = rows[:, :ROWS]
        if carried is not None:
            low = low + carried
        carried = rows[:, ROWS:]
        pieces.append(low)
    return jnp.concatenate(pieces[::-1], axis=1)


def self_backward(heads, grad, logs, bias, kseg, qseg, bucket_table):
    length = heads.shape[1]
    pairs = H // 2
    return pl.pallas_call(
        functools.partial(backward_kernel, True),
        grid=(pairs,),
        in_specs=[
            squeezed(length, lambda p: (0, 0, p)),
            squeezed(length, lambda p: (1, 0, p)),
            squeezed(length, lambda p: (2, 0, p)),
            column(length),
            log_spec(length),
            bias_spec(length),
            whole((length, PAIR)),
            whole((length, PAIR)),
            whole((1, length)),
        ],
        out_specs=[
            pl.BlockSpec((3, length, PAIR), lambda p: (0, 0, p)),
            pl.BlockSpec((None, 8, SHARE), lambda p: (p, 0, 0)),
        ],
        out_shape=[
            jax.ShapeDtypeStruct((3, length, H * DK), bf16),
            jax.ShapeDtypeStruct((pairs, 8, SHARE), f32),
        ],
        scratch_shapes=[
            pltpu.VMEM((length, PAIR), f32),
            pltpu.VMEM((length, PAIR), f32),
            pltpu.VMEM((2, length, ROWS), f32),
        ],
        name="self_backward",
    )(heads, heads, heads, grad, logs, bias, kseg, qseg, bucket_table.reshape(1, length))


def cross_backward(query, pairs_kv, grad, logs):
    length = query.shape[0]
    states = pairs_kv.shape[1]
    pairs = H // 2
    return pl.pallas_call(
        functools.partial(backward_kernel, False),
        grid=(pairs,),
        in_specs=[
            column(length),
            squeezed(states, lambda p: (0, 0, p)),
            squeezed(states, lambda p: (1, 0, p)),
            column(length),
            log_spec(length),
        ],
        out_specs=[column(length), pl.BlockSpec((2, states, PAIR), lambda p: (0, 0, p))],
        out_shape=[
            jax.ShapeDtypeStruct((length, H * DK), bf16),
            jax.ShapeDtypeStruct((2, states, H * DK), bf16),
        ],
        scratch_shapes=[pltpu.VMEM((states, PAIR), f32), pltpu.VMEM((states, PAIR), f32)],
        name="cross_backward",
    )(query, pairs_kv, pairs_kv, grad, logs)


def call(kernel, grid, in_specs, out_specs, out_shape, scratch, name):
    return pl.pallas_call(
        kernel,
        grid=grid,
        in_specs=in_specs,
        out_specs=out_specs,
        out_shape=out_shape,
        scratch_shapes=scratch,
        name=name,
    )


def shape_of(shape, dtype):
    return jax.ShapeDtypeStruct(shape, dtype)


def rows_spec(rows, width):
    return pl.BlockSpec((rows, width), lambda i: (i, 0))


def fixed(shape):
    return pl.BlockSpec(shape, lambda *i: (0,) * len(shape))


def resident(shape):
    return pl.BlockSpec(
        shape, lambda *i: (0,) * len(shape), pipeline_mode=pl.Buffered(1)
    )


def scalars():
    return pl.BlockSpec(memory_space=pltpu.SMEM)


def part_of(me, step):
    return pl.ds(pl.multiple_of((me ^ step) * SHARE, SHARE), SHARE)


def norm_scale(values):
    return lax.rsqrt(jnp.mean(values * values, axis=-1, keepdims=True) + epsilon)


def norm_pull(values, gain, grad_normed):
    scale = norm_scale(values)
    weighted = grad_normed * gain
    pulled = scale * weighted - values * (
        scale * scale * scale * jnp.mean(weighted * values, axis=-1, keepdims=True)
    )
    return pulled, jnp.sum(grad_normed * values * scale, axis=0, keepdims=True)


def clear_first(*refs):
    @pl.when(pl.program_id(0) == 0)
    def _():
        for ref in refs:
            ref[...] = jnp.zeros_like(ref)


def pack_kernel(here_ref, attn_ref, out_ref, ffin_ref, ffout_ref, one, two, one_half, two_half):
    core = here_ref[1]
    inner = H * DK
    for at in range(2):
        one[inner * at : inner * (at + 1), :] = out_ref[at].astype(bf16)
    base = 2 * inner
    for matrix in range(3):
        for chunk in range(inner // SHARE):
            one[base : base + SHARE, :] = attn_ref[
                3 + matrix, :, SHARE * chunk : SHARE * (chunk + 1)
            ].astype(bf16)
            base += SHARE
    base = 0
    for matrix in range(2):
        for chunk in range(ffin_ref.shape[2] // SHARE):
            two[base : base + SHARE, :] = ffin_ref[
                matrix, :, SHARE * chunk : SHARE * (chunk + 1)
            ].astype(bf16)
            base += SHARE
    two[base:, :] = ffout_ref[...].astype(bf16)
    for full, half in ((one, one_half), (two, two_half)):
        rows = half.shape[0]
        half[...] = full[pl.ds(pl.multiple_of(core * rows, rows), rows), :]


def pack_weights(here, w_attn, w_attn_out, w_ff_in, w_ff_out):
    first = 5 * H * DK
    second = 3 * w_ff_in.shape[2]
    return pl.pallas_call(
        pack_kernel,
        in_specs=[scalars()] + [pl.BlockSpec(memory_space=pltpu.VMEM)] * 4,
        out_shape=[
            shape_of((first, SHARE), bf16),
            shape_of((second, SHARE), bf16),
            shape_of((first // 2, SHARE), bf16),
            shape_of((second // 2, SHARE), bf16),
        ],
        name="pack_weights",
    )(here, w_attn, w_attn_out, w_ff_in, w_ff_out)


def qkv_kernel(here_ref, x_ref, gains_ref, *refs):
    shares, (heads_ref, normed_ref, full_ref) = refs[:4], refs[4:]
    inner = H * DK

    @pl.when(pl.program_id(0) == 0)
    def _():
        for step in range(4):
            for matrix in range(3):
                full_ref[part_of(here_ref[0], step), inner * matrix : inner * (matrix + 1)] = (
                    shares[step][matrix]
                )

    values = x_ref[...].astype(f32)
    normed = (values * norm_scale(values) * gains_ref[0:1, :]).astype(bf16)
    normed_ref[...] = normed
    for matrix in range(3):
        heads_ref[matrix] = mm(
            normed, full_ref[:, inner * matrix : inner * (matrix + 1)]
        ).astype(bf16)


def qkv_forward(here, stream, gains, shares):
    tokens, width = stream.shape
    inner = H * DK
    return call(
        qkv_kernel,
        (tokens // ROWS,),
        [scalars(), rows_spec(ROWS, width), fixed(gains.shape)]
        + [fixed(share.shape) for share in shares],
        [
            pl.BlockSpec((3, ROWS, inner), lambda i: (0, i, 0)),
            rows_spec(ROWS, width),
            fixed((width, 3 * inner)),
        ],
        [
            shape_of((3, tokens, inner), bf16),
            shape_of((tokens, width), bf16),
            shape_of((width, 3 * inner), bf16),
        ],
        [],
        "qkv_forward",
    )(here, stream, gains, *shares)


def join_halves(here_ref, buffer, mine, other):
    rows = mine.shape[0]
    core = here_ref[1]
    buffer[pl.ds(pl.multiple_of(core * rows, rows), rows), :] = mine[...]
    buffer[pl.ds(pl.multiple_of((1 - core) * rows, rows), rows), :] = other[...]


def middle_kernel(here_ref, att_ref, x_ref, valid_ref, states_ref, gains_ref, own, m1, m2, m3,
                  o1, o2, o3, hidden_ref, normed_ref, query_ref, pairs_ref, sums_ref, wo_ref,
                  co_ref, full_ref, buffer):
    inner = H * DK
    clear_first(sums_ref)

    @pl.when(pl.program_id(0) == 0)
    def _():
        for step, pair in enumerate(((own, None), (m1, o1), (m2, o2), (m3, o3))):
            source = own
            if step:
                join_halves(here_ref, buffer, *pair)
                source = buffer
            place = part_of(here_ref[0], step)
            wo_ref[:, place] = source[0:inner, :]
            co_ref[:, place] = source[inner : 2 * inner, :]
            for chunk in range(3 * inner // SHARE):
                base = 2 * inner + SHARE * chunk
                full_ref[place, SHARE * chunk : SHARE * (chunk + 1)] = source[
                    base : base + SHARE, :
                ]

    stream = x_ref[...].astype(f32)
    valid = valid_ref[...]
    branch = mm(att_ref[...], wo_ref[...])
    hidden = stream + branch
    sums_ref[0:1, :] += jnp.sum(valid * (stream * stream), axis=0, keepdims=True)
    sums_ref[1:2, :] += jnp.sum(valid * (branch * branch), axis=0, keepdims=True)
    sums_ref[4:5, :] += jnp.sum(jnp.broadcast_to(valid, stream.shape), axis=0, keepdims=True)
    hidden_ref[...] = hidden
    normed = (hidden * norm_scale(hidden) * gains_ref[1:2, :]).astype(bf16)
    normed_ref[...] = normed
    query_ref[...] = mm(normed, full_ref[:, :inner]).astype(bf16)
    for at in range(2):
        pairs_ref[at] = mm(
            states_ref[...], full_ref[:, inner * (at + 1) : inner * (at + 2)]
        ).astype(bf16)


def middle_forward(here, attended, stream, valid, states, gains, own, mine, other):
    tokens, width = stream.shape
    inner = H * DK
    steps = tokens // ROWS
    state_rows = states.shape[0] // steps
    return call(
        middle_kernel,
        (steps,),
        [
            scalars(),
            rows_spec(ROWS, inner),
            rows_spec(ROWS, width),
            rows_spec(ROWS, 1),
            rows_spec(state_rows, width),
            fixed(gains.shape),
            resident(own.shape),
        ]
        + [resident(mine[0].shape)] * 6,
        [
            rows_spec(ROWS, width),
            rows_spec(ROWS, width),
            rows_spec(ROWS, inner),
            pl.BlockSpec((2, state_rows, inner), lambda i: (0, i, 0)),
            fixed((8, width)),
            fixed((inner, width)),
            fixed((inner, width)),
            fixed((width, 3 * inner)),
        ],
        [
            shape_of((tokens, width), f32),
            shape_of((tokens, width), bf16),
            shape_of((tokens, inner), bf16),
            shape_of((2, states.shape[0], inner), bf16),
            shape_of((8, width), f32),
            shape_of((inner, width), bf16),
            shape_of((inner, width), bf16),
            shape_of((width, 3 * inner), bf16),
        ],
        [pltpu.VMEM(own.shape, bf16)],
        "middle_forward",
    )(here, attended, stream, valid, states, gains, own, *mine, *other)


gelu_scale = 0.7978845608028654
gelu_cubic = 0.044715


def outer_kernel(here_ref, att_ref, hidden_ref, valid_ref, cot_ref, gains_ref, co_ref, own, m1,
                 m2, m3, o1, o2, o3, output_ref, grad_ref, att_grad_ref, sums_ref, gain_ref,
                 mine_ref, s1, s2, s3, buffer, up_ref, down_ref, up_sum, down_sum, out_sum):
    hidden_units = down_ref.shape[0]
    clear_first(sums_ref, gain_ref, up_sum, down_sum, out_sum)

    @pl.when(pl.program_id(0) == 0)
    def _():
        for step, pair in enumerate(((own, None), (m1, o1), (m2, o2), (m3, o3))):
            source = own
            if step:
                join_halves(here_ref, buffer, *pair)
                source = buffer
            place = part_of(here_ref[0], step)
            for chunk in range(2 * hidden_units // SHARE):
                up_ref[place, SHARE * chunk : SHARE * (chunk + 1)] = source[
                    SHARE * chunk : SHARE * (chunk + 1), :
                ]
            down_ref[:, place] = source[2 * hidden_units :, :]

    valid = valid_ref[...]
    attended = att_ref[...]
    branch = mm(attended, co_ref[...])
    hidden = hidden_ref[...] + branch
    sums_ref[2:3, :] += jnp.sum(valid * (branch * branch), axis=0, keepdims=True)
    gain = gains_ref[2:3, :]
    normed = (hidden * norm_scale(hidden) * gain).astype(bf16)
    gate = mm(normed, up_ref[:, :hidden_units])
    upward = mm(normed, up_ref[:, hidden_units:])
    square = gate * gate
    bend = jnp.tanh(gelu_scale * (gate + gelu_cubic * (square * gate)))
    half = 0.5 * (1.0 + bend)
    curved = gate * half
    slope = half + 0.5 * gate * (1.0 - bend * bend) * (
        gelu_scale * (1.0 + 3.0 * gelu_cubic * square)
    )
    active = (curved * upward).astype(bf16)
    branch = mm(active, down_ref[...])
    sums_ref[3:4, :] += jnp.sum(valid * (branch * branch), axis=0, keepdims=True)
    output_ref[...] = (hidden + branch).astype(bf16)
    grad_out = cot_ref[...].astype(f32) * valid
    grad_low = grad_out.astype(bf16)
    down_sum[...] += mm(active, grad_low, TN)
    grad_active = mm(grad_low, down_ref[...], NT)
    grad_gate = (grad_active * upward * slope).astype(bf16)
    grad_upward = (grad_active * curved).astype(bf16)
    up_sum[:, :hidden_units] += mm(normed, grad_gate, TN)
    up_sum[:, hidden_units:] += mm(normed, grad_upward, TN)
    grad_normed = mm(grad_gate, up_ref[:, :hidden_units], NT) + mm(
        grad_upward, up_ref[:, hidden_units:], NT
    )
    pulled, gain_grad = norm_pull(hidden, gain, grad_normed)
    gain_ref[0:1, :] += gain_grad
    grad_hidden = grad_out + pulled
    grad_ref[...] = grad_hidden
    grad_low = grad_hidden.astype(bf16)
    out_sum[...] += mm(attended, grad_low, TN)
    att_grad_ref[...] = mm(grad_low, co_ref[...], NT).astype(bf16)

    @pl.when(pl.program_id(0) == pl.num_programs(0) - 1)
    def _():
        for step, target in enumerate((mine_ref, s1, s2, s3)):
            place = part_of(here_ref[0], step)
            kind = target.dtype
            for chunk in range(2 * hidden_units // SHARE):
                target[SHARE * chunk : SHARE * (chunk + 1), :] = up_sum[
                    place, SHARE * chunk : SHARE * (chunk + 1)
                ].astype(kind)
            target[2 * hidden_units : 3 * hidden_units, :] = down_sum[:, place].astype(kind)
            target[3 * hidden_units :, :] = out_sum[:, place].astype(kind)


def outer_layer(here, attended, hidden, valid, cotangent, gains, co_full, own, mine, other):
    tokens, width = hidden.shape
    inner = H * DK
    units = own.shape[0] // 3
    send = (3 * units + inner, SHARE)
    return call(
        outer_kernel,
        (tokens // ROWS,),
        [
            scalars(),
            rows_spec(ROWS, inner),
            rows_spec(ROWS, width),
            rows_spec(ROWS, 1),
            rows_spec(ROWS, width),
            fixed(gains.shape),
            resident(co_full.shape),
            resident(own.shape),
        ]
        + [resident(mine[0].shape)] * 6,
        [
            rows_spec(ROWS, width),
            rows_spec(ROWS, width),
            rows_spec(ROWS, inner),
            fixed((8, width)),
            fixed((8, width)),
        ]
        + [resident(send)] * 4,
        [
            shape_of((tokens, width), bf16),
            shape_of((tokens, width), f32),
            shape_of((tokens, inner), bf16),
            shape_of((8, width), f32),
            shape_of((8, width), f32),
            shape_of(send, f32),
        ]
        + [shape_of(send, bf16)] * 3,
        [
            pltpu.VMEM(own.shape, bf16),
            pltpu.VMEM((width, 2 * units), bf16),
            pltpu.VMEM((units, width), bf16),
            pltpu.VMEM((width, 2 * units), f32),
            pltpu.VMEM((units, width), f32),
            pltpu.VMEM((inner, width), f32),
        ],
        "outer_layer",
    )(here, attended, hidden, valid, cotangent, gains, co_full, own, *mine, *other)


def inner_kernel(here_ref, query_grad_ref, hidden_ref, normed_ref, att_ref, grad_ref, pair_ref,
                 states_ref, gains_ref, wo_ref, full_ref, grad1_ref, att_grad_ref, states_grad_ref,
                 gain_ref, mine_ref, s1, s2, s3, out_sum, full_sum):
    inner = H * DK
    clear_first(gain_ref, out_sum, full_sum)
    query_grad = query_grad_ref[...]
    grad_normed = mm(query_grad, full_ref[:, :inner], NT)
    pulled, gain_grad = norm_pull(hidden_ref[...], gains_ref[1:2, :], grad_normed)
    gain_ref[0:1, :] += gain_grad
    grad_hidden = grad_ref[...] + pulled
    grad1_ref[...] = grad_hidden
    grad_low = grad_hidden.astype(bf16)
    out_sum[...] += mm(att_ref[...], grad_low, TN)
    att_grad_ref[...] = mm(grad_low, wo_ref[...], NT).astype(bf16)
    full_sum[:, :inner] += mm(normed_ref[...], query_grad, TN)
    total = None
    for at in range(2):
        columns = slice(inner * (at + 1), inner * (at + 2))
        full_sum[:, columns] += mm(states_ref[...], pair_ref[at], TN)
        piece = mm(pair_ref[at], full_ref[:, columns], NT)
        total = piece if total is None else total + piece
    states_grad_ref[...] = total

    @pl.when(pl.program_id(0) == pl.num_programs(0) - 1)
    def _():
        for step, target in enumerate((mine_ref, s1, s2, s3)):
            place = part_of(here_ref[0], step)
            kind = target.dtype
            target[:inner, :] = out_sum[:, place].astype(kind)
            for chunk in range(3 * inner // SHARE):
                base = inner + SHARE * chunk
                target[base : base + SHARE, :] = full_sum[
                    place, SHARE * chunk : SHARE * (chunk + 1)
                ].astype(kind)


def inner_backward(here, query_grad, hidden, normed, attended, grad, pair_grad, states, gains,
                   wo_full, full):
    tokens, width = hidden.shape
    inner = H * DK
    steps = tokens // ROWS
    state_rows = states.shape[0] // steps
    send = (4 * inner, SHARE)
    return call(
        inner_kernel,
        (steps,),
        [
            scalars(),
            rows_spec(ROWS, inner),
            rows_spec(ROWS, width),
            rows_spec(ROWS, width),
            rows_spec(ROWS, inner),
            rows_spec(ROWS, width),
            pl.BlockSpec((2, state_rows, inner), lambda i: (0, i, 0)),
            rows_spec(state_rows, width),
            fixed(gains.shape),
            resident(wo_full.shape),
            resident(full.shape),
        ],
        [
            rows_spec(ROWS, width),
            rows_spec(ROWS, inner),
            rows_spec(state_rows, width),
            fixed((8, width)),
        ]
        + [resident(send)] * 4,
        [
            shape_of((tokens, width), f32),
            shape_of((tokens, inner), bf16),
            shape_of(states.shape, f32),
            shape_of((8, width), f32),
            shape_of(send, f32),
        ]
        + [shape_of(send, bf16)] * 3,
        [pltpu.VMEM((inner, width), f32), pltpu.VMEM((width, 3 * inner), f32)],
        "inner_backward",
    )(here, query_grad, hidden, normed, attended, grad, pair_grad, states, gains, wo_full, full)


def weights_kernel(here_ref, heads_ref, normed_ref, mine_ref, s1, s2, s3, full_sum):
    inner = H * DK
    clear_first(full_sum)
    normed = normed_ref[...]
    for matrix in range(3):
        full_sum[:, inner * matrix : inner * (matrix + 1)] += mm(normed, heads_ref[matrix], TN)

    @pl.when(pl.program_id(0) == pl.num_programs(0) - 1)
    def _():
        for step, target in enumerate((mine_ref, s1, s2, s3)):
            place = part_of(here_ref[0], step)
            for chunk in range(3 * inner // SHARE):
                target[SHARE * chunk : SHARE * (chunk + 1), :] = full_sum[
                    place, SHARE * chunk : SHARE * (chunk + 1)
                ].astype(target.dtype)


def qkv_weights(here, head_grads, normed):
    tokens, width = normed.shape
    inner = H * DK
    send = (3 * inner, SHARE)
    return call(
        weights_kernel,
        (tokens // ROWS,),
        [
            scalars(),
            pl.BlockSpec((3, ROWS, inner), lambda i: (0, i, 0)),
            rows_spec(ROWS, width),
        ],
        [resident(send)] * 4,
        [shape_of(send, f32)] + [shape_of(send, bf16)] * 3,
        [pltpu.VMEM((width, 3 * inner), f32)],
        "qkv_weights",
    )(here, head_grads, normed)


def last_kernel(here_ref, heads_ref, x_ref, grad_ref, gains_ref, full_ref, table_ref, gain1_ref,
                gain2_ref, sums1_ref, sums2_ref, out_ref, mine_ref, s1, s2, s3, gain_sum):
    inner = H * DK
    clear_first(gain_sum)
    grad_normed = None
    for matrix in range(3):
        piece = mm(heads_ref[matrix], full_ref[:, inner * matrix : inner * (matrix + 1)], NT)
        grad_normed = piece if grad_normed is None else grad_normed + piece
    pulled, gain_grad = norm_pull(x_ref[...].astype(f32), gains_ref[0:1, :], grad_normed)
    gain_sum[0:1, :] += gain_grad
    out_ref[...] = grad_ref[...] + pulled

    @pl.when(pl.program_id(0) == pl.num_programs(0) - 1)
    def _():
        table = [table_ref[at, 0:2, :] for at in range(H // 2)]
        sums = sums1_ref[...] + sums2_ref[...]
        folded = sums[:, :SHARE]
        for chunk in range(1, sums.shape[1] // SHARE):
            folded = folded + sums[:, SHARE * chunk : SHARE * (chunk + 1)]
        upper = folded.astype(bf16).astype(f32)
        for step, target in enumerate((mine_ref, s1, s2, s3)):
            place = part_of(here_ref[0], step)
            target[...] = jnp.concatenate(
                [gain_sum[0:1, place], gain1_ref[0:1, place], gain2_ref[0:1, place],
                 jnp.zeros((5, SHARE), f32)]
                + table
                + [jnp.zeros((8 - H, SHARE), f32), upper, folded - upper],
                axis=0,
            ).astype(target.dtype)


def last_backward(here, head_grads, stream, grad, gains, full, table, gain1, gain2, sums1, sums2):
    tokens, width = stream.shape
    inner = H * DK
    send = (32, SHARE)
    return call(
        last_kernel,
        (tokens // ROWS,),
        [
            scalars(),
            pl.BlockSpec((3, ROWS, inner), lambda i: (0, i, 0)),
            rows_spec(ROWS, width),
            rows_spec(ROWS, width),
            fixed(gains.shape),
            resident(full.shape),
            fixed(table.shape),
            fixed(gain1.shape),
            fixed(gain2.shape),
            fixed(sums1.shape),
            fixed(sums2.shape),
        ],
        [rows_spec(ROWS, width)] + [resident(send)] * 4,
        [shape_of((tokens, width), f32), shape_of(send, f32)] + [shape_of(send, bf16)] * 3,
        [pltpu.VMEM((8, width), f32)],
        "last_backward",
    )(here, head_grads, stream, grad, gains, full, table, gain1, gain2, sums1, sums2)


def exact(left, right, dims):
    return lax.dot_general(
        left, right, dims, precision=highest, preferred_element_type=f32
    )


def gathered_sum(refs, first, rows):
    total = refs[0][first : first + rows, :]
    for ref in refs[1:]:
        total = total + ref[first : first + rows, :].astype(f32)
    return total


def tail_kernel(*refs):
    fs, cs = refs[0:4], refs[4:8]
    attn_err, out_err, ffin_err, ffout_err, start_ref = refs[8:13]
    part_ref, out_grad, ffin_grad, ffout_grad, left_ref = refs[13:]
    inner = H * DK
    units = ffout_err.shape[0]
    at = 0
    for matrix in range(3):
        pieces = [
            gathered_sum(cs, inner + inner * matrix + SHARE * chunk, SHARE)
            for chunk in range(inner // SHARE)
        ]
        share = jnp.concatenate(pieces, axis=1)
        part_ref[matrix] = share
        left_ref[:, at : at + inner] = exact(
            start_ref[3 + matrix], share + attn_err[3 + matrix], TN
        )
        at += inner
    for matrix in range(2):
        share = gathered_sum(cs, 0, inner) if matrix == 0 else gathered_sum(fs, 3 * units, inner)
        out_grad[matrix] = share
        left_ref[:, at : at + inner] = exact(
            start_ref[6 + matrix], share + out_err[matrix], (((0,), (1,)), ((), ()))
        )
        at += inner
    for matrix in range(2):
        pieces = [
            gathered_sum(fs, units * matrix + SHARE * chunk, SHARE)
            for chunk in range(units // SHARE)
        ]
        share = jnp.concatenate(pieces, axis=1)
        ffin_grad[matrix] = share
        left_ref[:, at : at + units] = exact(
            start_ref[8 + matrix], share + ffin_err[matrix], TN
        )
        at += units
    share = gathered_sum(fs, 2 * units, units)
    ffout_grad[...] = share
    left_ref[:, at : at + units] = exact(
        start_ref[10], share + ffout_err[...], (((0,), (1,)), ((), ()))
    )


def tail_first(fs, cs, errors, start):
    inner = H * DK
    units = errors[3].shape[0]
    return pl.pallas_call(
        tail_kernel,
        out_shape=[
            shape_of((3, SHARE, inner), f32),
            shape_of((2, inner, SHARE), f32),
            shape_of((2, SHARE, units), f32),
            shape_of((units, SHARE), f32),
            shape_of((8, 5 * inner + 3 * units), f32),
        ],
        name="tail_first",
    )(*fs, *cs, *errors, start)


def tail_qkv_kernel(*refs):
    qs, ts = refs[0:4], refs[4:8]
    attn_err, start_ref, part_ref, grad_ref, left_ref = refs[8:]
    inner = H * DK
    for matrix in range(3):
        pieces = [
            gathered_sum(qs, inner * matrix + SHARE * chunk, SHARE)
            for chunk in range(inner // SHARE)
        ]
        share = jnp.concatenate(pieces, axis=1)
        grad_ref[matrix] = share
        grad_ref[3 + matrix] = part_ref[matrix]
        left_ref[:, inner * matrix : inner * (matrix + 1)] = exact(
            start_ref[matrix], share + attn_err[matrix], TN
        )
    small = gathered_sum(ts, 0, 32)
    base = 3 * inner
    left_ref[:, base : base + SHARE] = small[0:8]
    left_ref[:, base + SHARE : base + 2 * SHARE] = small[8:16]
    left_ref[:, base + 2 * SHARE :] = small[16:24] + small[24:32]


def tail_qkv(qs, ts, attn_err, start, part):
    inner = H * DK
    return pl.pallas_call(
        tail_qkv_kernel,
        out_shape=[
            shape_of(attn_err.shape, f32),
            shape_of((8, 3 * inner + 3 * SHARE), f32),
        ],
        name="tail_qkv",
    )(*qs, *ts, attn_err, start, part)


def orthonormal(current):
    row = lax.broadcasted_iota(jnp.int32, (current.shape[0], 1), 0)
    for column in range(current.shape[0]):
        line = current[column : column + 1]
        line = line * lax.rsqrt(jnp.sum(line * line, axis=1, keepdims=True) + epsilon)
        dots = jnp.sum(current * line, axis=1, keepdims=True)
        later = current - dots * line
        current = jnp.where(row > column, later, jnp.where(row == column, line, current))
    return current


def matrices(inner, units):
    listed = []
    base = 0
    for group, count, width in ((0, 6, inner), (1, 2, inner), (2, 2, units), (3, 1, units)):
        for at in range(count):
            listed.append((group, at, base, width))
            base += width
    return listed


def spot_of(group, at):
    return slice(None) if group == 3 else at


def right_kernel(replicas, listed, groups, total_ref, *refs):
    count = len(groups)
    grads = dict(zip(groups, refs[:count]))
    errors = dict(zip(groups, refs[count : 2 * count]))
    left_ref, right_ref = refs[2 * count :]
    for index, (group, at, base, width) in enumerate(listed):
        columns = slice(base - listed[0][2], base - listed[0][2] + width)
        left = orthonormal(total_ref[:, columns] * (1.0 / replicas))
        left_ref[:, columns] = left
        spot = spot_of(group, at)
        merged = grads[group][spot] + errors[group][spot]
        right_ref[8 * index : 8 * (index + 1), :] = exact(
            left, merged, NN if group in (1, 3) else NT
        )


def tail_right(replicas, listed, total, grads, errors):
    groups = tuple(sorted(set(item[0] for item in listed)))
    lanes = sum(item[3] for item in listed)
    return pl.pallas_call(
        functools.partial(right_kernel, replicas, listed, groups),
        out_shape=[shape_of((8, lanes), f32), shape_of((8 * len(listed), SHARE), f32)],
        name="tail_right",
    )(total, *[grads[group] for group in groups], *[errors[group] for group in groups])


def final_kernel(replicas, listed, groups, more, *refs):
    rights, lefts, refs = refs[0:more], refs[more : 2 * more], refs[2 * more :]
    count = len(groups)
    grads, errors, moments, new_errors, new_moments, updates = (
        dict(zip(groups, refs[count * at : count * (at + 1)])) for at in range(6)
    )
    factor_ref = refs[6 * count]
    for place, (source, row, base, group, at, width) in enumerate(listed):
        mean = rights[source][8 * row : 8 * (row + 1), :] * (1.0 / replicas)
        factor_ref[place] = mean.T
        left = lefts[source][:, base : base + width]
        change = exact(left, mean, TN) if group in (1, 3) else exact(mean, left, TN)
        spot = spot_of(group, at)
        new_errors[group][spot] = grads[group][spot] + errors[group][spot] - change
        moment = decay * moments[group][spot] + change
        new_moments[group][spot] = moment
        updates[group][spot] = -rates[group] * moment


def tail_final(replicas, listed, rights, lefts, grads, errors, moments):
    groups = tuple(sorted(set(item[3] for item in listed)))
    picked = [table[group] for table in (grads, errors, moments) for group in groups]
    shapes = [shape_of(moments[group].shape, f32) for group in groups]
    return pl.pallas_call(
        functools.partial(final_kernel, replicas, listed, groups, len(rights)),
        out_shape=shapes * 3 + [shape_of((len(listed), SHARE, 8), f32)],
        name="tail_final",
    )(*rights, *lefts, *picked)


def swap(value, axis, bit):
    size = lax.axis_size(axis)
    return lax.ppermute(value, axis, [(at, at ^ bit) for at in range(size)])


def sum_over(value, axis):
    bit = 1
    while bit < lax.axis_size(axis):
        value = value + swap(value, axis, bit)
        bit *= 2
    return value


def after(value, *others):
    return lax.optimization_barrier((value,) + others)[0]


def body(
    block_input,
    cotangent,
    encoder_states,
    segment_ids,
    bucket_table,
    w_attn,
    w_attn_out,
    w_ff_in,
    w_ff_out,
    norm_gains,
    rel_bias,
    mom_attn,
    mom_attn_out,
    mom_ff_in,
    mom_ff_out,
    mom_gains,
    mom_bias,
    err_attn,
    err_attn_out,
    err_ff_in,
    err_ff_out,
    q_start,
):
    length, width = block_input.shape[1:]
    replicas = lax.axis_size("rep")
    owners = lax.axis_size("grp")
    buckets = rel_bias.shape[0] * owners
    group = lax.axis_index("grp")
    here = jnp.stack([group, lax.axis_index("rep") % 2]).astype(jnp.int32)
    stream = block_input[0]
    states = encoder_states[0]
    segment = segment_ids[0]
    valid = (segment > 0).astype(f32)[:, None]

    small = jnp.concatenate(
        [norm_gains, jnp.pad(rel_bias, ((0, 0), (0, SHARE - H))), jnp.zeros((5, SHARE), f32)],
        axis=0,
    ).astype(bf16)
    smalls = [small] + [swap(small, "grp", step) for step in range(1, owners)]
    stacked = jnp.stack(smalls)
    ordered = jnp.stack(
        [lax.dynamic_index_in_dim(stacked, group ^ owner, 0, False) for owner in range(owners)]
    )
    gains = ordered[:, 0:3].transpose(1, 0, 2).reshape(3, width).astype(f32)
    table_low = ordered[:, 3:11, :H].reshape(buckets, H)
    first = w_attn[0:3].astype(bf16)
    first_shares = [first] + [
        swap(after(first, smalls[-1]), "grp", step) for step in range(1, owners)
    ]
    one, two, one_half, two_half = pack_weights(here, w_attn, w_attn_out, w_ff_in, w_ff_out)
    bias = bias_tiles(bucket_table, table_low)
    one_hot = segment[:, None] == jnp.arange(PAIR)[None, :]
    kseg = one_hot.astype(bf16)
    known = jnp.arange(PAIR)[None, :] < 8
    qseg = jnp.where(known & ~one_hot, masked_score, 0.0).astype(bf16)
    one_half, bias, *first_shares = lax.optimization_barrier((one_half, bias, *first_shares))
    one_mine = [swap(one_half, "grp", step) for step in range(1, owners)]

    heads, normed0, qkv_full = qkv_forward(here, stream, gains, first_shares)
    attended, self_logs = self_forward(heads, bias, kseg, qseg)
    attended, two_half, *one_mine = lax.optimization_barrier((attended, two_half, *one_mine))
    one_other = [swap(part, "rep", 1) for part in one_mine]
    two_mine = [swap(two_half, "grp", step) for step in range(1, owners)]
    hidden1, normed1, cross_query, cross_pairs, sums1, wo_full, co_full, cross_full = middle_forward(
        here, attended, stream, valid, states, gains, one, one_mine, one_other
    )
    cross_attended, cross_logs = cross_forward(cross_query, cross_pairs)
    cross_attended, *two_mine = lax.optimization_barrier((cross_attended, *two_mine))
    two_other = [swap(part, "rep", 1) for part in two_mine]
    (block_output, grad_h2, grad_cross_att, sums2, gain2, f_own, *f_sends) = outer_layer(
        here, cross_attended, hidden1, valid, cotangent[0], gains, co_full, two, two_mine, two_other
    )
    f_parts = [swap(part, "grp", step) for step, part in zip(range(1, owners), f_sends)]
    grad_cross_query, grad_cross_pairs = cross_backward(
        cross_query, cross_pairs, grad_cross_att, cross_logs
    )
    (grad_h1, grad_attended, encoder_grad, gain1, c_own, *c_sends) = inner_backward(
        here, grad_cross_query, hidden1, normed1, attended, grad_h2, grad_cross_pairs, states, gains,
        wo_full, cross_full,
    )
    c_parts = [swap(part, "grp", step) for step, part in zip(range(1, owners), c_sends)]
    head_grads, table_parts = self_backward(
        heads, grad_attended, self_logs, bias, kseg, qseg, bucket_table
    )
    q_own, *q_sends = qkv_weights(here, head_grads, normed0)
    q_parts = [swap(part, "grp", step) for step, part in zip(range(1, owners), q_sends)]
    (input_grad, t_own, *t_sends) = last_backward(
        here, head_grads, stream, grad_h1, gains, qkv_full, table_parts, gain1, gain2, sums1, sums2
    )
    t_parts = [swap(part, "grp", step) for step, part in zip(range(1, owners), t_sends)]

    errors = (err_attn[0], err_attn_out[0], err_ff_in[0], err_ff_out[0])
    moments = (mom_attn, mom_attn_out, mom_ff_in, mom_ff_out)
    part, out_grad, ffin_grad, ffout_grad, left_two = tail_first(
        [f_own] + f_parts, [c_own] + c_parts, errors, q_start
    )
    left_two = sum_over(left_two, "rep")
    attn_grad, left_one = tail_qkv(
        [q_own] + q_parts, [t_own] + t_parts, errors[0], q_start, part
    )
    base = 3 * H * DK
    share_gains = left_one[0:3, base : base + SHARE]
    table_sum = left_one[0:H, base + SHARE : base + SHARE + buckets]
    share_bias = lax.dynamic_slice_in_dim(
        table_sum, group * (buckets // owners), buckets // owners, 1
    ).T
    left_one = sum_over(left_one, "rep")
    mean_gains = left_one[0:3, base : base + SHARE] / replicas
    mean_bias = lax.dynamic_slice_in_dim(
        left_one[0:H, base + SHARE : base + SHARE + buckets] / replicas,
        group * (buckets // owners), buckets // owners, 1,
    ).T
    totals = jnp.sum(left_one[0:5, base + 2 * SHARE :], axis=1)
    branch_rms = jnp.sqrt(totals[0:4] / totals[4])
    listed = matrices(H * DK, w_ff_out.shape[0])
    later = (part, out_grad, ffin_grad, ffout_grad)
    late_list = [(group, at - 3 if group == 0 else at, at_lane, lanes)
                 for group, at, at_lane, lanes in listed[3:]]
    late_errors = (err_attn[0, 3:], *errors[1:])
    left_late, right_late = tail_right(replicas, late_list, left_two, later, late_errors)
    right_late = sum_over(right_late, "rep")
    grads = (attn_grad, out_grad, ffin_grad, ffout_grad)
    finals_late = tail_final(
        replicas,
        [(0, 3 + place, item[2] - base, item[0], item[1], item[3])
         for place, item in enumerate(listed[6:])],
        [right_late], [left_late], grads, errors, moments,
    )
    left_early, right_early = tail_right(replicas, listed[:3], left_one, grads, errors)
    right_early = sum_over(right_early, "rep")
    finals = tail_final(
        replicas,
        [(0, place, item[2], item[0], item[1], item[3]) for place, item in enumerate(listed[:3])]
        + [(1, place, item[2] - base, item[0], item[1], item[3])
           for place, item in enumerate(listed[3:6])],
        [right_early, right_late], [left_early, left_late], grads, errors, moments,
    )
    gain_moment = decay * mom_gains + mean_gains
    bias_moment = decay * mom_bias + mean_bias
    return (
        block_output[None],
        input_grad[None],
        encoder_grad[None],
        branch_rms,
        attn_grad[None],
        out_grad[None],
        ffin_grad[None],
        ffout_grad[None],
        share_gains[None],
        share_bias[None],
        finals[0][None],
        finals_late[0][None],
        finals_late[1][None],
        finals_late[2][None],
        finals[1],
        finals_late[3],
        finals_late[4],
        finals_late[5],
        gain_moment,
        bias_moment,
        finals[2],
        finals_late[6],
        finals_late[7],
        finals_late[8],
        -rates[4] * gain_moment,
        -rates[5] * bias_moment,
        jnp.concatenate([finals[3], finals_late[9]], axis=0),
    )


def solution(mesh):
    in_specs = (
        P(("grp", "rep"), None, None),
        P(("grp", "rep"), None, None),
        P(("grp", "rep"), None, None),
        P(("grp", "rep"), None),
        P(),
        P(None, "grp", None),
        P(None, None, "grp"),
        P(None, "grp", None),
        P(None, "grp"),
        P(None, "grp"),
        P("grp", None),
        P(None, "grp", None),
        P(None, None, "grp"),
        P(None, "grp", None),
        P(None, "grp"),
        P(None, "grp"),
        P("grp", None),
        P("rep", None, "grp", None),
        P("rep", None, None, "grp"),
        P("rep", None, "grp", None),
        P("rep", None, "grp"),
        P(None, "grp", None),
    )
    out_specs = (
        P(("grp", "rep"), None, None),
        P(("grp", "rep"), None, None),
        P(("grp", "rep"), None, None),
        P(),
        P("rep", None, "grp", None),
        P("rep", None, None, "grp"),
        P("rep", None, "grp", None),
        P("rep", None, "grp"),
        P("rep", None, "grp"),
        P("rep", "grp", None),
        P("rep", None, "grp", None),
        P("rep", None, None, "grp"),
        P("rep", None, "grp", None),
        P("rep", None, "grp"),
        P(None, "grp", None),
        P(None, None, "grp"),
        P(None, "grp", None),
        P(None, "grp"),
        P(None, "grp"),
        P("grp", None),
        P(None, "grp", None),
        P(None, None, "grp"),
        P(None, "grp", None),
        P(None, "grp"),
        P(None, "grp"),
        P("grp", None),
        P(None, "grp", None),
    )
    return jax.shard_map(body, mesh=mesh, in_specs=in_specs, out_specs=out_specs, check_vma=False)
```

profile of v0, /device:TPU:0, one launch (start us, length us, event | category | flops | bytes accessed | tf_op | source)
XLA Modules:
  0.0 284.5 jit_solution(2160994371762871408)
XLA Ops:
  2.2 3.9 %collective-permute-start.2 = (bf16[16,128]{1,0:T(8,128)(2,1)S(1)}, bf16[16,128]{1,0:T(8,128)(2,1)S(1)}, u32[]{:S(2)}, u32[]{:S(2)}) collective-permute-start(bf16[16,128]{1,0:T(8,128)(2,1)S(1)} %maximum_maximum_fusion), channel_id=1, source_target_pairs={{0,24},{8,16},{16,8},{24,0},{1,25},{9,17},{17,9},{25,1},{2,26},{10... | collective-permute-start | bytes 12296 | tf_op jit(solution)/shard_map/ppermute | solution.py:1029
  11.6 3.3 %pack_weights.1 = (bf16[1920,128]{1,0:T(8,128)(2,1)}, bf16[3072,128]{1,0:T(8,128)(2,1)}, bf16[960,128]{1,0:T(8,128)(2,1)}, bf16[1536,128]{1,0:T(8,128)(2,1)}) custom-call(s32[2]{0:T(128)} %pad_add_fusion.here_ref, f32[6,128,384]{2,1,0:T(8,128)} %attn_ref.1, f32[2,384,128]{2,1,0:T(8,128)} %out_ref.1, f32[2,128,1024]{2,1,0:T(8,128)} %ffin_ref.1, ...), custom_call_target="tpu_custom_call" | custom-call | tf_op jit(solution)/shard_map/pack_weights/pallas_call | solution.py:397
  19.0 9.9 %bias_tiles.1.refs_3_.refs_5_ = f32[6,1024,256]{2,1,0:T(8,128)} custom-call(s32[1,1024]{1,0:T(1,128)} %bitcast.74, bf16[32,6]{1,0:T(8,128)(2,1)} %fusion.3.table_ref), custom_call_target="tpu_custom_call" | custom-call | tf_op jit(solution)/shard_map/bias_tiles/pallas_call | solution.py:56
  35.8 6.6 %qkv_forward.1 = (bf16[3,1024,384]{2,1,0:T(8,128)(2,1)}, bf16[1024,512]{1,0:T(8,128)(2,1)}, bf16[512,1152]{1,0:T(8,128)(2,1)}) custom-call(s32[2]{0:T(128)} %pad_add_fusion.here_ref, bf16[1024,512]{1,0:T(8,128)(2,1)} %bitcast.53, f32[3,512]{1,0:T(4,128)} %convert_bitcast_fusion.gains_ref, bf16[3,128,384]{2,1,0:T(8,128)(2,1)} %copy-done.1, ...), custom_call_target="tpu_custom_call" | custom-call | tf_op jit(solution)/shard_map/qkv_forward/pallas_call | solution.py:434
  42.4 14.7 %self_forward.1 = (bf16[1024,384]{1,0:T(8,128)(2,1)}, f32[3,8,1024]{2,1,0:T(8,128)}) custom-call(bf16[3,1024,384]{2,1,0:T(8,128)(2,1)} %get-tuple-element.123.refs_0_.refs_1_.refs_2_, bf16[3,1024,384]{2,1,0:T(8,128)(2,1)} %get-tuple-element.123.refs_0_.refs_1_.refs_2_, bf16[3,1024,384]{2,1,0:T(8,128)(2,1)} %get-tuple-element.123.refs_0_.refs_1_.refs_2_, ...), custom_call_target="tpu_custom_call" | custom-call | tf_op jit(solution)/shard_map/self_forward/pallas_call | solution.py:136
  63.4 7.6 %middle_forward.1 = (f32[1024,512]{1,0:T(8,128)}, bf16[1024,512]{1,0:T(8,128)(2,1)}, bf16[1024,384]{1,0:T(8,128)(2,1)}, bf16[2,512,384]{2,1,0:T(8,128)(2,1)}, f3...) custom-call(s32[2]{0:T(128)} %pad_add_fusion.here_ref, ...), custom_call_target="tpu_custom_call" | custom-call | tf_op jit(solution)/shard_map/middle_forward/pallas_call | solution.py:505
  70.9 14.0 %cross_forward.1 = (bf16[1024,384]{1,0:T(8,128)(2,1)}, f32[3,8,1024]{2,1,0:T(8,128)}) custom-call(bf16[1024,384]{1,0:T(8,128)(2,1)} %get-tuple-element.133.refs_0_, bf16[2,512,384]{2,1,0:T(8,128)(2,1)} %get-tuple-element.134.refs_1_.refs_2_, bf16[2,512,384]{2,1,0:T(8,128)(2,1)} %get-tuple-element.134.refs_1_.refs_2_), custom_call_target="tpu_custom_call" | custom-call | tf_op jit(solution)/shard_map/cross_forward/pallas_call | solution.py:160
  88.7 22.7 %outer_layer.1 = (bf16[1024,512]{1,0:T(8,128)(2,1)}, f32[1024,512]{1,0:T(8,128)}, bf16[1024,384]{1,0:T(8,128)(2,1)}, f32[8,512]{1,0:T(8,128)}, f32[8,512]{1,0:T(...) custom-call(s32[2]{0:T(128)} %pad_add_fusion.here_ref, ...), custom_call_target="tpu_custom_call" | custom-call | tf_op jit(solution)/shard_map/outer_layer/pallas_call | solution.py:624
  112.6 14.1 %cross_backward.1 = (bf16[1024,384]{1,0:T(8,128)(2,1)}, bf16[2,512,384]{2,1,0:T(8,128)(2,1)}) custom-call(bf16[1024,384]{1,0:T(8,128)(2,1)} %get-tuple-element.133.refs_0_, bf16[2,512,384]{2,1,0:T(8,128)(2,1)} %get-tuple-element.134.refs_1_.refs_2_, bf16[2,512,384]{2,1,0:T(8,128)(2,1)} %get-tuple-element.134.refs_1_.refs_2_, ...), custom_call_target="tpu_custom_call" | custom-call | tf_op jit(solution)/shard_map/cross_backward/pallas_call | solution.py:291
  126.7 10.3 %inner_backward.1 = (f32[1024,512]{1,0:T(8,128)}, bf16[1024,384]{1,0:T(8,128)(2,1)}, f32[512,512]{1,0:T(8,128)}, f32[8,512]{1,0:T(8,128)}, f32[1536,128]{1,0:T(8...) custom-call(s32[2]{0:T(128)} %pad_add_fusion.here_ref, ...), custom_call_target="tpu_custom_call" | custom-call | tf_op jit(solution)/shard_map/inner_backward/pallas_call | solution.py:710
  140.6 22.8 %self_backward.1 = (bf16[3,1024,384]{2,1,0:T(8,128)(2,1)}, f32[3,8,128]{2,1,0:T(8,128)}) custom-call(bf16[3,1024,384]{2,1,0:T(8,128)(2,1)} %get-tuple-element.123.refs_0_.refs_1_.refs_2_, bf16[3,1024,384]{2,1,0:T(8,128)(2,1)} %get-tuple-element.123.refs_0_.refs_1_.refs_2_, bf16[3,1024,384]{2,1,0:T(8,128)(2,1)} %get-tuple-element.123.refs_0_.refs_1_.refs_2_, ...), custom_call_target="tpu_custom_call" | custom-call | tf_op jit(solution)/shard_map/self_backward/pallas_call | solution.py:256
  163.4 6.6 %last_backward.1 = (f32[1024,512]{1,0:T(8,128)}, f32[32,128]{1,0:T(8,128)}, bf16[32,128]{1,0:T(8,128)(2,1)}, bf16[32,128]{1,0:T(8,128)(2,1)}, bf16[32,128]{1,0:T(8,128)(2,1)}) custom-call(s32[2]{0:T(128)} %pad_add_fusion.here_ref, bf16[3,1024,384]{2,1,0:T(8,128)(2,1)} %get-tuple-element.155.heads_ref, bf16[1024,512]{1,0:T(8,128)(2,1)} %bitcast.55, ...), custom_call_target="tpu_custom_call" | custom-call | tf_op jit(solution)/shard_map/last_backward/pallas_call | solution.py:817
  170.9 3.0 %collective-permute-done.21.refs_5_ = bf16[32,128]{1,0:T(8,128)(2,1)S(1)} collective-permute-done((bf16[32,128]{1,0:T(8,128)(2,1)}, bf16[32,128]{1,0:T(8,128)(2,1)S(1)}, u32[]{:S(2)}, u32[]{:S(2)}) %collective-permute-start.21) | collective-permute-done | bytes 8224 | tf_op jit(solution)/shard_map/ppermute | solution.py:1029
  176.2 5.9 %qkv_weights.1 = (f32[1152,128]{1,0:T(8,128)}, bf16[1152,128]{1,0:T(8,128)(2,1)}, bf16[1152,128]{1,0:T(8,128)(2,1)}, bf16[1152,128]{1,0:T(8,128)(2,1)}) custom-call(s32[2]{0:T(128)} %pad_add_fusion.here_ref, bf16[3,1024,384]{2,1,0:T(8,128)(2,1)} %get-tuple-element.155.heads_ref, bf16[1024,512]{1,0:T(8,128)(2,1)} %get-tuple-element.165.normed_ref), custom_call_target="tpu_custom_call" | custom-call | tf_op jit(solution)/shard_map/qkv_weights/pallas_call | solution.py:767
  182.1 13.1 %collective-permute-done.28.refs_6_ = bf16[1536,128]{1,0:T(8,128)(2,1)S(1)} collective-permute-done((bf16[1536,128]{1,0:T(8,128)(2,1)}, bf16[1536,128]{1,0:T(8,128)(2,1)S(1)}, u32[]{:S(2)}, u32[]{:S(2)}) %collective-permute-start.28) | collective-permute-done | bytes 393248 | tf_op jit(solution)/shard_map/ppermute | solution.py:1029
  202.6 6.4 %tail_first.1 = (f32[3,128,384]{2,1,0:T(8,128)}, f32[2,384,128]{2,1,0:T(8,128)}, f32[2,128,1024]{2,1,0:T(8,128)}, f32[1024,128]{1,0:T(8,128)}, f32[8,4992]{1,0:T(8,128)}) custom-call(f32[3456,128]{1,0:T(8,128)} %get-tuple-element.174.refs_0_, bf16[3456,128]{1,0:T(8,128)(2,1)} %copy-done.2, bf16[3456,128]{1,0:T(8,128)(2,1)} %copy-done.3, ...), custom_call_target="tpu_custom_call" | custom-call | tf_op jit(solution)/shard_map/tail_first/pallas_call | solution.py:899
  211.3 3.6 %tail_qkv.1 = (f32[6,128,384]{2,1,0:T(8,128)}, f32[8,1536]{1,0:T(8,128)}) custom-call(f32[1152,128]{1,0:T(8,128)} %get-tuple-element.166.refs_0_, bf16[1152,128]{1,0:T(8,128)(2,1)} %copy-done.16, bf16[1152,128]{1,0:T(8,128)(2,1)} %collective-permute-done.19.refs_2_, bf16[1152,128]{1,0:T(8,128)(2,1)} %collective-permute-done.20.refs_3_, ...), custom_call_target="tpu_custom_call" | custom-call | tf_op jit(solution)/shard_map/tail_qkv/pallas_call | solution.py:936
  226.3 4.3 %tail_right.2 = (f32[8,1152]{1,0:T(8,128)}, f32[24,128]{1,0:T(8,128)}) custom-call(f32[8,1536]{1,0:T(8,128)} %add.72.total_ref, f32[6,128,384]{2,1,0:T(8,128)} %get-tuple-element.184.refs_0_.refs_4_, f32[6,128,384]{2,1,0:T(8,128)} %bitcast.51), custom_call_target="tpu_custom_call" | custom-call | tf_op jit(solution)/shard_map/tail_right/pallas_call | solution.py:990
  233.1 4.2 %collective-permute-done.37 = f32[8,4992]{1,0:T(8,128)S(1)} collective-permute-done((f32[8,4992]{1,0:T(8,128)S(1)}, f32[8,4992]{1,0:T(8,128)S(1)}, u32[]{:S(2)}, u32[]{:S(2)}) %collective-permute-start.37) | collective-permute-done | bytes 159776 | tf_op jit(solution)/shard_map/ppermute | solution.py:1029
  237.3 2.9 %collective-permute-start.38 = (f32[8,4992]{1,0:T(8,128)S(1)}, f32[8,4992]{1,0:T(8,128)S(1)}, u32[]{:S(2)}, u32[]{:S(2)}) collective-permute-start(f32[8,4992]{1,0:T(8,128)S(1)} %add.78), channel_id=1, source_target_pairs={{0,4},{1,5},{2,6},{3,7},{4,0},{5,1},{6,2},{7,3},{8,12},{9,13},{10,... | collective-permute-start | bytes 479240 | tf_op jit(solution)/shard_map/ppermute | solution.py:1029
  240.3 7.5 %collective-permute-done.38 = f32[8,4992]{1,0:T(8,128)S(1)} collective-permute-done((f32[8,4992]{1,0:T(8,128)S(1)}, f32[8,4992]{1,0:T(8,128)S(1)}, u32[]{:S(2)}, u32[]{:S(2)}) %collective-permute-start.38) | collective-permute-done | bytes 159776 | tf_op jit(solution)/shard_map/ppermute | solution.py:1029
  248.5 7.3 %tail_right.3 = (f32[8,4992]{1,0:T(8,128)}, f32[64,128]{1,0:T(8,128)}) custom-call(f32[8,4992]{1,0:T(8,128)} %add.79.total_ref, f32[3,128,384]{2,1,0:T(8,128)} %get-tuple-element.182.refs_10_.refs_0_, f32[2,384,128]{2,1,0:T(8,128)} %get-tuple-element.185.refs_1_.refs_2_, f32[2,128,1024]{2,1,0:T(8,128)} %get-tuple-element.186.refs_2_.refs_3_, ...), custom_call_target="tpu_custom_call" | custom-call | tf_op jit(solution)/shard_map/tail_right/pallas_call | solution.py:990
  269.7 6.6 %tail_final.3 = (f32[2,384,128]{2,1,0:T(8,128)}, f32[2,128,1024]{2,1,0:T(8,128)}, f32[1024,128]{1,0:T(8,128)}, f32[2,384,128]{2,1,0:T(8,128)}, f32[2,128,1024]{2...) custom-call(f32[64,128]{1,0:T(8,128)} %add.82.refs_1_.refs_0_, ...), custom_call_target="tpu_custom_call" | custom-call | tf_op jit(solution)/shard_map/tail_final/pallas_call | solution.py:1020
  277.4 5.1 %tail_final.2 = (f32[6,128,384]{2,1,0:T(8,128)}, f32[6,128,384]{2,1,0:T(8,128)}, f32[6,128,384]{2,1,0:T(8,128)}, f32[6,128,8]{2,1,0:T(8,128)}) custom-call(f32[24,128]{1,0:T(8,128)} %add.76.refs_0_, f32[64,128]{1,0:T(8,128)} %add.82.refs_1_.refs_0_, f32[8,1152]{1,0:T(8,128)} %get-tuple-element.191.refs_2_, f32[8,4992]{1,0:T(8,128)} %get-tuple-element.192.refs_3_.refs_1_, ...), custom_call_target="tpu_custom_call" | custom-call | tf_op jit(solution)/shard_map/tail_final/pallas_call | solution.py:1020
  (203 shorter events, 76.7 us)
Async XLA Ops:
  2.2 12.6 %collective-permute-start.2 = (bf16[16,128]{1,0:T(8,128)(2,1)S(1)}, bf16[16,128]{1,0:T(8,128)(2,1)S(1)}, u32[]{:S(2)}, u32[]{:S(2)}) collective-permute-start(bf16[16,128]{1,0:T(8,128)(2,1)S(1)} %maximum_maximum_fusion), channel_id=1, source_target_pairs={{0,24},{8,16},{16,8},{24,0},{1,25},{9,17},{17,9},{25,1},{2,26},{10... | collective-permute-start | bytes 12296 | tf_op jit(solution)/shard_map/ppermute | solution.py:1029
  6.1 12.2 %collective-permute-start = (bf16[16,128]{1,0:T(8,128)(2,1)S(1)}, bf16[16,128]{1,0:T(8,128)(2,1)S(1)}, u32[]{:S(2)}, u32[]{:S(2)}) collective-permute-start(bf16[16,128]{1,0:T(8,128)(2,1)S(1)} %maximum_maximum_fusion), channel_id=1, source_target_pairs={{0,8},{8,0},{16,24},{24,16},{1,9},{9,1},{17,25},{25,17},{2,10},{10... | collective-permute-start | bytes 12296 | tf_op jit(solution)/shard_map/ppermute | solution.py:1029
  6.7 11.7 %collective-permute-start.1 = (bf16[16,128]{1,0:T(8,128)(2,1)S(1)}, bf16[16,128]{1,0:T(8,128)(2,1)S(1)}, u32[]{:S(2)}, u32[]{:S(2)}) collective-permute-start(bf16[16,128]{1,0:T(8,128)(2,1)S(1)} %maximum_maximum_fusion), channel_id=1, source_target_pairs={{0,16},{8,24},{16,0},{24,8},{1,17},{9,25},{17,1},{25,9},{2,18},{10... | collective-permute-start | bytes 12296 | tf_op jit(solution)/shard_map/ppermute | solution.py:1029
  14.8 14.1 %collective-permute-start.3 = (bf16[3,128,384]{2,1,0:T(8,128)(2,1)S(1)}, bf16[3,128,384]{2,1,0:T(8,128)(2,1)S(1)}, u32[]{:S(2)}, u32[]{:S(2)}) collective-permute-start(bf16[3,128,384]{2,1,0:T(8,128)(2,1)S(1)} %slice.58.refs_0_), channel_id=1, source_target_pairs={{0,8},{8,0},{16,24},{24,16},{1,9},{9,1},{17,25},{25,17},{2,10},{10... | collective-permute-start | bytes 884744 | tf_op jit(solution)/shard_map/ppermute | solution.py:1029
  16.7 13.9 %collective-permute-start.4 = (bf16[3,128,384]{2,1,0:T(8,128)(2,1)S(1)}, bf16[3,128,384]{2,1,0:T(8,128)(2,1)S(1)}, u32[]{:S(2)}, u32[]{:S(2)}) collective-permute-start(bf16[3,128,384]{2,1,0:T(8,128)(2,1)S(1)} %slice.58.refs_0_), channel_id=1, source_target_pairs={{0,16},{8,24},{16,0},{24,8},{1,17},{9,25},{17,1},{25,9},{2,18},{10... | collective-permute-start | bytes 884744 | tf_op jit(solution)/shard_map/ppermute | solution.py:1029
  18.3 12.4 %collective-permute-start.5 = (bf16[3,128,384]{2,1,0:T(8,128)(2,1)S(1)}, bf16[3,128,384]{2,1,0:T(8,128)(2,1)S(1)}, u32[]{:S(2)}, u32[]{:S(2)}) collective-permute-start(bf16[3,128,384]{2,1,0:T(8,128)(2,1)S(1)} %slice.58.refs_0_), channel_id=1, source_target_pairs={{0,24},{8,16},{16,8},{24,0},{1,25},{9,17},{17,9},{25,1},{2,26},{10... | collective-permute-start | bytes 884744 | tf_op jit(solution)/shard_map/ppermute | solution.py:1029
  30.7 26.4 %collective-permute-start.6 = (bf16[960,128]{1,0:T(8,128)(2,1)S(1)}, bf16[960,128]{1,0:T(8,128)(2,1)S(1)}, u32[]{:S(2)}, u32[]{:S(2)}) collective-permute-start(bf16[960,128]{1,0:T(8,128)(2,1)S(1)} %copy-done.34), channel_id=1, source_target_pairs={{0,8},{8,0},{16,24},{24,16},{1,9},{9,1},{17,25},{25,17},{2,10},{10... | collective-permute-start | bytes 737288 | tf_op jit(solution)/shard_map/ppermute | solution.py:1029
  31.9 25.2 %collective-permute-start.7 = (bf16[960,128]{1,0:T(8,128)(2,1)S(1)}, bf16[960,128]{1,0:T(8,128)(2,1)S(1)}, u32[]{:S(2)}, u32[]{:S(2)}) collective-permute-start(bf16[960,128]{1,0:T(8,128)(2,1)S(1)} %copy-done.34), channel_id=1, source_target_pairs={{0,16},{8,24},{16,0},{24,8},{1,17},{9,25},{17,1},{25,9},{2,18},{10... | collective-permute-start | bytes 737288 | tf_op jit(solution)/shard_map/ppermute | solution.py:1029
  32.8 24.3 %collective-permute-start.8 = (bf16[960,128]{1,0:T(8,128)(2,1)S(1)}, bf16[960,128]{1,0:T(8,128)(2,1)S(1)}, u32[]{:S(2)}, u32[]{:S(2)}) collective-permute-start(bf16[960,128]{1,0:T(8,128)(2,1)S(1)} %copy-done.34), channel_id=1, source_target_pairs={{0,24},{8,16},{16,8},{24,0},{1,25},{9,17},{17,9},{25,1},{2,26},{10... | collective-permute-start | bytes 737288 | tf_op jit(solution)/shard_map/ppermute | solution.py:1029
  57.2 27.7 %collective-permute-start.12 = (bf16[1536,128]{1,0:T(8,128)(2,1)S(1)}, bf16[1536,128]{1,0:T(8,128)(2,1)S(1)}, u32[]{:S(2)}, u32[]{:S(2)}) collective-permute-start(bf16[1536,128]{1,0:T(8,128)(2,1)S(1)} %copy-done.33), channel_id=1, source_target_pairs={{0,8},{8,0},{16,24},{24,16},{1,9},{9,1},{17,25},{25,17},{2,10},{10... | collective-permute-start | bytes 1179656 | tf_op jit(solution)/shard_map/ppermute | solution.py:1029
  58.5 26.5 %collective-permute-start.13 = (bf16[1536,128]{1,0:T(8,128)(2,1)S(1)}, bf16[1536,128]{1,0:T(8,128)(2,1)S(1)}, u32[]{:S(2)}, u32[]{:S(2)}) collective-permute-start(bf16[1536,128]{1,0:T(8,128)(2,1)S(1)} %copy-done.33), channel_id=1, source_target_pairs={{0,16},{8,24},{16,0},{24,8},{1,17},{9,25},{17,1},{25,9},{2,18},{10... | collective-permute-start | bytes 1179656 | tf_op jit(solution)/shard_map/ppermute | solution.py:1029
  59.4 25.7 %collective-permute-start.14 = (bf16[1536,128]{1,0:T(8,128)(2,1)S(1)}, bf16[1536,128]{1,0:T(8,128)(2,1)S(1)}, u32[]{:S(2)}, u32[]{:S(2)}) collective-permute-start(bf16[1536,128]{1,0:T(8,128)(2,1)S(1)} %copy-done.33), channel_id=1, source_target_pairs={{0,24},{8,16},{16,8},{24,0},{1,25},{9,17},{17,9},{25,1},{2,26},{10... | collective-permute-start | bytes 1179656 | tf_op jit(solution)/shard_map/ppermute | solution.py:1029
  111.4 85.8 %collective-permute-start.24 = (bf16[3456,128]{1,0:T(8,128)(2,1)}, bf16[3456,128]{1,0:T(8,128)(2,1)S(1)}, u32[]{:S(2)}, u32[]{:S(2)}) collective-permute-start(bf16[3456,128]{1,0:T(8,128)(2,1)} %get-tuple-element.175), channel_id=1, source_target_pairs={{0,8},{8,0},{16,24},{24,16},{1,9},{9,1},{17,25},{25,17},{2,10},{10... | collective-permute-start | bytes 2654216 | tf_op jit(solution)/shard_map/ppermute | solution.py:1029
  137.0 37.7 %collective-permute-start.27 = (bf16[1536,128]{1,0:T(8,128)(2,1)}, bf16[1536,128]{1,0:T(8,128)(2,1)S(1)}, u32[]{:S(2)}, u32[]{:S(2)}) collective-permute-start(bf16[1536,128]{1,0:T(8,128)(2,1)} %get-tuple-element.179), channel_id=1, source_target_pairs={{0,8},{8,0},{16,24},{24,16},{1,9},{9,1},{17,25},{25,17},{2,10},{10... | collective-permute-start | bytes 1179656 | tf_op jit(solution)/shard_map/ppermute | solution.py:1029
  138.0 60.7 %collective-permute-start.25 = (bf16[3456,128]{1,0:T(8,128)(2,1)}, bf16[3456,128]{1,0:T(8,128)(2,1)S(1)}, u32[]{:S(2)}, u32[]{:S(2)}) collective-permute-start(bf16[3456,128]{1,0:T(8,128)(2,1)} %get-tuple-element.176), channel_id=1, source_target_pairs={{0,16},{8,24},{16,0},{24,8},{1,17},{9,25},{17,1},{25,9},{2,18},{10... | collective-permute-start | bytes 2654216 | tf_op jit(solution)/shard_map/ppermute | solution.py:1029
  139.5 60.8 %collective-permute-start.26 = (bf16[3456,128]{1,0:T(8,128)(2,1)}, bf16[3456,128]{1,0:T(8,128)(2,1)S(1)}, u32[]{:S(2)}, u32[]{:S(2)}) collective-permute-start(bf16[3456,128]{1,0:T(8,128)(2,1)} %get-tuple-element.177), channel_id=1, source_target_pairs={{0,24},{8,16},{16,8},{24,0},{1,25},{9,17},{17,9},{25,1},{2,26},{10... | collective-permute-start | bytes 2654216 | tf_op jit(solution)/shard_map/ppermute | solution.py:1029
  173.8 21.3 %collective-permute-start.28 = (bf16[1536,128]{1,0:T(8,128)(2,1)}, bf16[1536,128]{1,0:T(8,128)(2,1)S(1)}, u32[]{:S(2)}, u32[]{:S(2)}) collective-permute-start(bf16[1536,128]{1,0:T(8,128)(2,1)} %get-tuple-element.180), channel_id=1, source_target_pairs={{0,16},{8,24},{16,0},{24,8},{1,17},{9,25},{17,1},{25,9},{2,18},{10... | collective-permute-start | bytes 1179656 | tf_op jit(solution)/shard_map/ppermute | solution.py:1029
  174.8 21.6 %collective-permute-start.29 = (bf16[1536,128]{1,0:T(8,128)(2,1)}, bf16[1536,128]{1,0:T(8,128)(2,1)}, u32[]{:S(2)}, u32[]{:S(2)}) collective-permute-start(bf16[1536,128]{1,0:T(8,128)(2,1)} %get-tuple-element.181), channel_id=1, source_target_pairs={{0,24},{8,16},{16,8},{24,0},{1,25},{9,17},{17,9},{25,1},{2,26},{10... | collective-permute-start | bytes 1179656 | tf_op jit(solution)/shard_map/ppermute | solution.py:1029
  195.2 15.4 %collective-permute-start.18 = (bf16[1152,128]{1,0:T(8,128)(2,1)}, bf16[1152,128]{1,0:T(8,128)(2,1)S(1)}, u32[]{:S(2)}, u32[]{:S(2)}) collective-permute-start(bf16[1152,128]{1,0:T(8,128)(2,1)} %get-tuple-element.167), channel_id=1, source_target_pairs={{0,8},{8,0},{16,24},{24,16},{1,9},{9,1},{17,25},{25,17},{2,10},{10... | collective-permute-start | bytes 884744 | tf_op jit(solution)/shard_map/ppermute | solution.py:1029
  196.3 14.3 %collective-permute-start.19 = (bf16[1152,128]{1,0:T(8,128)(2,1)}, bf16[1152,128]{1,0:T(8,128)(2,1)}, u32[]{:S(2)}, u32[]{:S(2)}) collective-permute-start(bf16[1152,128]{1,0:T(8,128)(2,1)} %get-tuple-element.168), channel_id=1, source_target_pairs={{0,16},{8,24},{16,0},{24,8},{1,17},{9,25},{17,1},{25,9},{2,18},{10... | collective-permute-start | bytes 884744 | tf_op jit(solution)/shard_map/ppermute | solution.py:1029
  197.2 13.4 %collective-permute-start.20 = (bf16[1152,128]{1,0:T(8,128)(2,1)}, bf16[1152,128]{1,0:T(8,128)(2,1)}, u32[]{:S(2)}, u32[]{:S(2)}) collective-permute-start(bf16[1152,128]{1,0:T(8,128)(2,1)} %get-tuple-element.169), channel_id=1, source_target_pairs={{0,24},{8,16},{16,8},{24,0},{1,25},{9,17},{17,9},{25,1},{2,26},{10... | collective-permute-start | bytes 884744 | tf_op jit(solution)/shard_map/ppermute | solution.py:1029
  216.0 14.7 %collective-permute-start.36 = (f32[8,4992]{1,0:T(8,128)S(1)}, f32[8,4992]{1,0:T(8,128)S(1)}, u32[]{:S(2)}, u32[]{:S(2)}) collective-permute-start(f32[8,4992]{1,0:T(8,128)S(1)} %copy-done.23), channel_id=1, source_target_pairs={{0,1},{1,0},{2,3},{3,2},{4,5},{5,4},{6,7},{7,6},{8,9},{9,8},{10,11... | collective-permute-start | bytes 479240 | tf_op jit(solution)/shard_map/ppermute | solution.py:1029
  230.7 26.4 %collective-permute-start.33 = (f32[24,128]{1,0:T(8,128)}, f32[24,128]{1,0:T(8,128)S(1)}, u32[]{:S(2)}, u32[]{:S(2)}) collective-permute-start(f32[24,128]{1,0:T(8,128)} %get-tuple-element.188), channel_id=1, source_target_pairs={{0,1},{1,0},{2,3},{3,2},{4,5},{5,4},{6,7},{7,6},{8,9},{9,8},{10,11... | collective-permute-start | bytes 36872 | tf_op jit(solution)/shard_map/ppermute | solution.py:1029
  237.3 10.5 %collective-permute-start.38 = (f32[8,4992]{1,0:T(8,128)S(1)}, f32[8,4992]{1,0:T(8,128)S(1)}, u32[]{:S(2)}, u32[]{:S(2)}) collective-permute-start(f32[8,4992]{1,0:T(8,128)S(1)} %add.78), channel_id=1, source_target_pairs={{0,4},{1,5},{2,6},{3,7},{4,0},{5,1},{6,2},{7,3},{8,12},{9,13},{10,... | collective-permute-start | bytes 479240 | tf_op jit(solution)/shard_map/ppermute | solution.py:1029
  (55 other events, 308.2 us)
where the time goes:
time: 289 us; the launch traced here: 285 us
  Pallas kernels  172 us (60%)
  starting transfers between devices  46.9 us (16%)
  waiting for transfers between devices  37.3 us (13%)
  other arithmetic  13.9 us (5%)
  local copies, waits for them, and re-layouts  13.3 us (5%)
    ppermute x42, starting transfers between devices, swap(): return lax.ppermute(value, axis, [(at, at ^ bit) for at in range(size)])  46.9 us
    ppermute x42, waiting for transfers between devices, swap(): return lax.ppermute(value, axis, [(at, at ^ bit) for at in range(size)])  37.3 us
    pallas_call x1, Pallas kernels, self_backward(): pl.pallas_call(functools.partial(backward_kernel, True), grid=(pairs,), i...  22.8 us
    pallas_call x1, Pallas kernels, outer_layer(): call(outer_kernel, (tokens // ROWS,), [scalars(), rows_spec(ROWS, inner),...  22.7 us
    pallas_call x1, Pallas kernels, self_forward(): pl.pallas_call(functools.partial(forward_kernel, True), grid=(pairs,), in...  14.7 us
    pallas_call x1, Pallas kernels, cross_backward(): pl.pallas_call(functools.partial(backward_kernel, False), grid=(pairs,),...  14.1 us
    pallas_call x1, Pallas kernels, cross_forward(): pl.pallas_call(functools.partial(forward_kernel, False), grid=(pairs,), i...  14 us
    pallas_call x2, Pallas kernels, tail_final(): pl.pallas_call(functools.partial(final_kernel, replicas, listed, groups,...  11.7 us
  transfers between devices with their start and end apart: 42, of which 12 were waited for; matrix products, arithmetic and copies ran while one was open for 7% of the time, Pallas kernels for 47%

commit v1 on v0

--- a/solution.py
+++ b/solution.py
@@ -7,17 +7,18 @@
 from jax.experimental.pallas import tpu as pltpu
 from jax.sharding import PartitionSpec as P
 
+
 H = 6
 DK = 64
 PAIR = 2 * DK
 ROWS = 256
 SHARE = 128
+TILE = 512
 
 epsilon = 1e-06
 decay = 0.5
 rates = (0.002, 0.5, 0.015, 0.015, 0.005, 0.05)
 masked_score = -1e30
-highest = lax.Precision.HIGHEST
 NT = (((1,), (1,)), ((), ()))
 NN = (((1,), (0,)), ((), ()))
 TN = (((0,), (0,)), ((), ()))
@@ -94,20 +95,29 @@
     values = turned(v_ref[...])
     masks = lane_masks(ROWS)
     log_ref[...] = jnp.zeros_like(log_ref)
+
+    def start(first):
+        count = first + ROWS if causal else keys.shape[0]
+        return [
+            scores_of(q_ref, keys, bias_ref, qseg_ref, first, count, half, masks[half])[1]
+            for half in range(2)
+        ]
+
+    scores = start(0)
     for first in range(0, length, ROWS):
-        count = first + ROWS if causal else keys.shape[0]
-        mixed = []
+        tops = [jnp.max(score, axis=0, keepdims=True) for score in scores]
+        ahead = start(first + ROWS) if first + ROWS < length else None
+        powers = [jnp.exp(score - top) for score, top in zip(scores, tops)]
+        totals = [jnp.sum(power, axis=0, keepdims=True) for power in powers]
+        probs = [(power * (1.0 / total)).astype(bf16) for power, total in zip(powers, totals)]
+        mixed = [
+            mm(values[DK * half : DK * (half + 1), : probs[half].shape[0]], probs[half])
+            for half in range(2)
+        ]
         for half in range(2):
-            unused, scores = scores_of(
-                q_ref, keys, bias_ref, qseg_ref, first, count, half, masks[half]
-            )
-            top = jnp.max(scores, axis=0, keepdims=True)
-            powers = jnp.exp(scores - top)
-            total = jnp.sum(powers, axis=0, keepdims=True)
-            probs = (powers * (1.0 / total)).astype(bf16)
-            mixed.append(mm(values[DK * half : DK * (half + 1), :count], probs))
-            log_ref[half : half + 1, first : first + ROWS] = top + jnp.log(total)
+            log_ref[half : half + 1, first : first + ROWS] = tops[half] + jnp.log(totals[half])
         out_ref[first : first + ROWS, :] = jnp.concatenate(mixed, axis=0).T.astype(bf16)
+        scores = ahead
 
 
 def squeezed(rows, index):
@@ -190,24 +200,49 @@
     masks = lane_masks(ROWS)
     key_sum[...] = jnp.zeros_like(key_sum)
     value_sum[...] = jnp.zeros_like(value_sum)
-    for first in range(0, length, ROWS):
+
+    def start(first):
         count = first + ROWS if causal else states
-        query_grads = []
+        begun = []
         for half in range(2):
             query, scores = scores_of(
                 q_ref, keys, bias_ref, qseg_ref, first, count, half, masks[half]
             )
-            probs = jnp.exp(scores - log_ref[half : half + 1, first : first + ROWS])
             grad = grad_ref[first : first + ROWS, :]
             grad = jnp.where(masks[half], grad, jnp.zeros_like(grad))
-            grad_probs = mm(v_ref[:count, :], grad, NT)
-            dots = jnp.sum(grad_probs * probs, axis=0, keepdims=True)
-            grad_scores = (probs * (grad_probs - dots)).astype(bf16)
-            value_sum[:count, :] += mm(probs.astype(bf16), grad)
-            key_sum[:count, :] += mm(grad_scores, query)
-            query_grads.append(mm(turned_keys[DK * half : DK * (half + 1), :count], grad_scores))
-            if causal:
-                tile_sum[half, length - count : length, :] += grad_scores.astype(f32)
+            begun.append((query, scores, grad, mm(v_ref[:count, :], grad, NT)))
+        return begun
+
+    begun = start(0)
+    for first in range(0, length, ROWS):
+        count = first + ROWS if causal else states
+        probs = [
+            jnp.exp(begun[half][1] - log_ref[half : half + 1, first : first + ROWS])
+            for half in range(2)
+        ]
+        ahead = start(first + ROWS) if first + ROWS < length else None
+        dots = [
+            jnp.sum(begun[half][3] * probs[half], axis=0, keepdims=True) for half in range(2)
+        ]
+        grad_scores = [
+            (probs[half] * (begun[half][3] - dots[half])).astype(bf16) for half in range(2)
+        ]
+        value_sum[:count, :] += mm(
+            jnp.concatenate([prob.astype(bf16) for prob in probs], axis=1),
+            jnp.concatenate([begun[0][2], begun[1][2]], axis=0),
+        )
+        key_sum[:count, :] += mm(
+            jnp.concatenate(grad_scores, axis=1),
+            jnp.concatenate([begun[0][0], begun[1][0]], axis=0),
+        )
+        query_grads = [
+            mm(turned_keys[DK * half : DK * (half + 1), :count], grad_scores[half])
+            for half in range(2)
+        ]
+        if causal:
+            for half in range(2):
+                tile_sum[half, length - count : length, :] += grad_scores[half].astype(f32)
+        begun = ahead
         joined = jnp.concatenate(query_grads, axis=0).T.astype(bf16)
         if causal:
             out_ref[0, first : first + ROWS, :] = joined
@@ -308,7 +343,7 @@
     )(query, pairs_kv, pairs_kv, grad, logs)
 
 
-def call(kernel, grid, in_specs, out_specs, out_shape, scratch, name):
+def call(kernel, grid, in_specs, out_specs, out_shape, scratch):
     return pl.pallas_call(
         kernel,
         grid=grid,
@@ -316,7 +351,6 @@
         out_specs=out_specs,
         out_shape=out_shape,
         scratch_shapes=scratch,
-        name=name,
     )
 
 
@@ -407,6 +441,15 @@
     )(here, w_attn, w_attn_out, w_ff_in, w_ff_out)
 
 
+def low_kernel(source_ref, out_ref):
+    out_ref[...] = source_ref[...].astype(bf16)
+
+
+def low_first(w_attn):
+    spec = pl.BlockSpec((1,) + w_attn.shape[1:], lambda i: (i, 0, 0))
+    return call(low_kernel, (3,), [spec], spec, shape_of((3,) + w_attn.shape[1:], bf16), [])(w_attn)
+
+
 def qkv_kernel(here_ref, x_ref, gains_ref, *refs):
     shares, (heads_ref, normed_ref, full_ref) = refs[:4], refs[4:]
     inner = H * DK
@@ -433,12 +476,12 @@
     inner = H * DK
     return call(
         qkv_kernel,
-        (tokens // ROWS,),
-        [scalars(), rows_spec(ROWS, width), fixed(gains.shape)]
+        (tokens // TILE,),
+        [scalars(), rows_spec(TILE, width), fixed(gains.shape)]
         + [fixed(share.shape) for share in shares],
         [
-            pl.BlockSpec((3, ROWS, inner), lambda i: (0, i, 0)),
-            rows_spec(ROWS, width),
+            pl.BlockSpec((3, TILE, inner), lambda i: (0, i, 0)),
+            rows_spec(TILE, width),
             fixed((width, 3 * inner)),
         ],
         [
@@ -447,7 +490,6 @@
             shape_of((width, 3 * inner), bf16),
         ],
         [],
-        "qkv_forward",
     )(here, stream, gains, *shares)
 
 
@@ -481,7 +523,7 @@
                 ]
 
     stream = x_ref[...].astype(f32)
-    valid = valid_ref[...]
+    valid = 1.0 - valid_ref[:, 0:1].astype(f32)
     branch = mm(att_ref[...], wo_ref[...])
     hidden = stream + branch
     sums_ref[0:1, :] += jnp.sum(valid * (stream * stream), axis=0, keepdims=True)
@@ -500,25 +542,25 @@
 def middle_forward(here, attended, stream, valid, states, gains, own, mine, other):
     tokens, width = stream.shape
     inner = H * DK
-    steps = tokens // ROWS
+    steps = tokens // TILE
     state_rows = states.shape[0] // steps
     return call(
         middle_kernel,
         (steps,),
         [
             scalars(),
-            rows_spec(ROWS, inner),
-            rows_spec(ROWS, width),
-            rows_spec(ROWS, 1),
+            rows_spec(TILE, inner),
+            rows_spec(TILE, width),
+            rows_spec(TILE, PAIR),
             rows_spec(state_rows, width),
             fixed(gains.shape),
             resident(own.shape),
         ]
         + [resident(mine[0].shape)] * 6,
         [
-            rows_spec(ROWS, width),
-            rows_spec(ROWS, width),
-            rows_spec(ROWS, inner),
+            rows_spec(TILE, width),
+            rows_spec(TILE, width),
+            rows_spec(TILE, inner),
             pl.BlockSpec((2, state_rows, inner), lambda i: (0, i, 0)),
             fixed((8, width)),
             fixed((inner, width)),
@@ -536,7 +578,6 @@
             shape_of((width, 3 * inner), bf16),
         ],
         [pltpu.VMEM(own.shape, bf16)],
-        "middle_forward",
     )(here, attended, stream, valid, states, gains, own, *mine, *other)
 
 
@@ -546,7 +587,8 @@
 
 def outer_kernel(here_ref, att_ref, hidden_ref, valid_ref, cot_ref, gains_ref, co_ref, own, m1,
                  m2, m3, o1, o2, o3, output_ref, grad_ref, att_grad_ref, sums_ref, gain_ref,
-                 mine_ref, s1, s2, s3, buffer, up_ref, down_ref, up_sum, down_sum, out_sum):
+                 mine_ref, to_x, to_y, keep_y, keep_x, buffer, up_ref, down_ref, up_sum, down_sum,
+                 out_sum):
     hidden_units = down_ref.shape[0]
     clear_first(sums_ref, gain_ref, up_sum, down_sum, out_sum)
 
@@ -564,7 +606,7 @@
                 ]
             down_ref[:, place] = source[2 * hidden_units :, :]
 
-    valid = valid_ref[...]
+    valid = 1.0 - valid_ref[:, 0:1].astype(f32)
     attended = att_ref[...]
     branch = mm(attended, co_ref[...])
     hidden = hidden_ref[...] + branch
@@ -605,15 +647,29 @@
 
     @pl.when(pl.program_id(0) == pl.num_programs(0) - 1)
     def _():
-        for step, target in enumerate((mine_ref, s1, s2, s3)):
-            place = part_of(here_ref[0], step)
-            kind = target.dtype
+        cut = keep_y.shape[0]
+
+        def fill(place, low, high, low_base, high_base):
+            def put(first, value):
+                if first < cut:
+                    if low is not None:
+                        at = low_base + first
+                        low[at : at + value.shape[0], :] = value.astype(low.dtype)
+                elif high is not None:
+                    at = high_base + first - cut
+                    high[at : at + value.shape[0], :] = value.astype(high.dtype)
+
             for chunk in range(2 * hidden_units // SHARE):
-                target[SHARE * chunk : SHARE * (chunk + 1), :] = up_sum[
-                    place, SHARE * chunk : SHARE * (chunk + 1)
-                ].astype(kind)
-            target[2 * hidden_units : 3 * hidden_units, :] = down_sum[:, place].astype(kind)
-            target[3 * hidden_units :, :] = out_sum[:, place].astype(kind)
+                put(SHARE * chunk, up_sum[place, SHARE * chunk : SHARE * (chunk + 1)])
+            put(2 * hidden_units, down_sum[:, place])
+            put(3 * hidden_units, out_sum[:, place])
+
+        me = here_ref[0]
+        high_rows = keep_x.shape[0]
+        fill(part_of(me, 0), mine_ref, mine_ref, 0, cut)
+        fill(part_of(me, 1), to_x, keep_x, 0, 0)
+        fill(part_of(me, 2), keep_y, to_y, 0, 0)
+        fill(part_of(me, 3), to_x, to_y, cut, high_rows)
 
 
 def outer_layer(here, attended, hidden, valid, cotangent, gains, co_full, own, mine, other):
@@ -621,6 +677,9 @@
     inner = H * DK
     units = own.shape[0] // 3
     send = (3 * units + inner, SHARE)
+    cut = units * 3 // 2 + SHARE
+    high = send[0] - cut
+    sends = [(2 * cut, SHARE), (2 * high, SHARE), (cut, SHARE), (high, SHARE)]
     return call(
         outer_kernel,
         (tokens // ROWS,),
@@ -628,7 +687,7 @@
             scalars(),
             rows_spec(ROWS, inner),
             rows_spec(ROWS, width),
-            rows_spec(ROWS, 1),
+            rows_spec(ROWS, PAIR),
             rows_spec(ROWS, width),
             fixed(gains.shape),
             resident(co_full.shape),
@@ -642,7 +701,7 @@
             fixed((8, width)),
             fixed((8, width)),
         ]
-        + [resident(send)] * 4,
+        + [resident(shape) for shape in [send] + sends],
         [
             shape_of((tokens, width), bf16),
             shape_of((tokens, width), f32),
@@ -651,7 +710,7 @@
             shape_of((8, width), f32),
             shape_of(send, f32),
         ]
-        + [shape_of(send, bf16)] * 3,
+        + [shape_of(shape, bf16) for shape in sends],
         [
             pltpu.VMEM(own.shape, bf16),
             pltpu.VMEM((width, 2 * units), bf16),
@@ -660,7 +719,6 @@
             pltpu.VMEM((units, width), f32),
             pltpu.VMEM((inner, width), f32),
         ],
-        "outer_layer",
     )(here, attended, hidden, valid, cotangent, gains, co_full, own, *mine, *other)
 
 
@@ -704,7 +762,7 @@
                    wo_full, full):
     tokens, width = hidden.shape
     inner = H * DK
-    steps = tokens // ROWS
+    steps = tokens // TILE
     state_rows = states.shape[0] // steps
     send = (4 * inner, SHARE)
     return call(
@@ -712,11 +770,11 @@
         (steps,),
         [
             scalars(),
-            rows_spec(ROWS, inner),
-            rows_spec(ROWS, width),
-            rows_spec(ROWS, width),
-            rows_spec(ROWS, inner),
-            rows_spec(ROWS, width),
+            rows_spec(TILE, inner),
+            rows_spec(TILE, width),
+            rows_spec(TILE, width),
+            rows_spec(TILE, inner),
+            rows_spec(TILE, width),
             pl.BlockSpec((2, state_rows, inner), lambda i: (0, i, 0)),
             rows_spec(state_rows, width),
             fixed(gains.shape),
@@ -724,8 +782,8 @@
             resident(full.shape),
         ],
         [
-            rows_spec(ROWS, width),
-            rows_spec(ROWS, inner),
+            rows_spec(TILE, width),
+            rows_spec(TILE, inner),
             rows_spec(state_rows, width),
             fixed((8, width)),
         ]
@@ -739,7 +797,6 @@
         ]
         + [shape_of(send, bf16)] * 3,
         [pltpu.VMEM((inner, width), f32), pltpu.VMEM((width, 3 * inner), f32)],
-        "inner_backward",
     )(here, query_grad, hidden, normed, attended, grad, pair_grad, states, gains, wo_full, full)
 
 
@@ -766,16 +823,15 @@
     send = (3 * inner, SHARE)
     return call(
         weights_kernel,
-        (tokens // ROWS,),
+        (tokens // TILE,),
         [
             scalars(),
-            pl.BlockSpec((3, ROWS, inner), lambda i: (0, i, 0)),
-            rows_spec(ROWS, width),
+            pl.BlockSpec((3, TILE, inner), lambda i: (0, i, 0)),
+            rows_spec(TILE, width),
         ],
         [resident(send)] * 4,
         [shape_of(send, f32)] + [shape_of(send, bf16)] * 3,
         [pltpu.VMEM((width, 3 * inner), f32)],
-        "qkv_weights",
     )(here, head_grads, normed)
 
 
@@ -816,12 +872,12 @@
     send = (32, SHARE)
     return call(
         last_kernel,
-        (tokens // ROWS,),
+        (tokens // TILE,),
         [
             scalars(),
-            pl.BlockSpec((3, ROWS, inner), lambda i: (0, i, 0)),
-            rows_spec(ROWS, width),
-            rows_spec(ROWS, width),
+            pl.BlockSpec((3, TILE, inner), lambda i: (0, i, 0)),
+            rows_spec(TILE, width),
+            rows_spec(TILE, width),
             fixed(gains.shape),
             resident(full.shape),
             fixed(table.shape),
@@ -830,16 +886,32 @@
             fixed(sums1.shape),
             fixed(sums2.shape),
         ],
-        [rows_spec(ROWS, width)] + [resident(send)] * 4,
+        [rows_spec(TILE, width)] + [resident(send)] * 4,
         [shape_of((tokens, width), f32), shape_of(send, f32)] + [shape_of(send, bf16)] * 3,
         [pltpu.VMEM((8, width), f32)],
-        "last_backward",
     )(here, head_grads, stream, grad, gains, full, table, gain1, gain2, sums1, sums2)
 
 
-def exact(left, right, dims):
-    return lax.dot_general(
-        left, right, dims, precision=highest, preferred_element_type=f32
+def split(value):
+    upper = value.astype(bf16)
+    return upper, (value - upper.astype(f32)).astype(bf16)
+
+
+def project(small, big, dims):
+    small_upper, small_lower = split(small)
+    big_upper, big_lower = split(big)
+    rows = small.shape[0]
+    product = mm(jnp.concatenate([small_upper, small_lower], axis=0), big_upper, dims)
+    return product[:rows] + product[rows:] + mm(small_upper, big_lower, dims)
+
+
+def outer_product(left, right):
+    left_upper, left_lower = split(left)
+    right_upper, right_lower = split(right)
+    return mm(
+        jnp.concatenate([left_upper, left_upper, left_lower], axis=0),
+        jnp.concatenate([right_upper, right_lower, right_upper], axis=0),
+        TN,
     )
 
 
@@ -850,97 +922,101 @@
     return total
 
 
+def joined_sum(refs, first, chunks):
+    pick = relayed_sum if len(refs) == 5 else gathered_sum
+    return jnp.concatenate(
+        [pick(refs, first + SHARE * chunk, SHARE) for chunk in range(chunks)], axis=1
+    )
+
+
+def relayed_sum(refs, first, rows):
+    own, from_x, next_y, from_y, next_x = refs
+    cut = next_y.shape[0]
+    pieces, at = ((from_x, next_y), first) if first < cut else ((from_y, next_x), first - cut)
+    total = own[first : first + rows, :]
+    for piece in pieces:
+        total = total + piece[at : at + rows, :].astype(f32)
+    return total
+
+
 def tail_kernel(*refs):
-    fs, cs = refs[0:4], refs[4:8]
-    attn_err, out_err, ffin_err, ffout_err, start_ref = refs[8:13]
-    part_ref, out_grad, ffin_grad, ffout_grad, left_ref = refs[13:]
+    fs, cs = refs[0:5], refs[5:9]
+    attn_err, out_err, ffin_err, ffout_err, start_ref = refs[9:14]
+    (part_ref, out_grad, ffin_grad, ffout_grad, part_sum, out_sum, ffin_sum, ffout_sum,
+     left_ref) = refs[14:]
     inner = H * DK
     units = ffout_err.shape[0]
     at = 0
     for matrix in range(3):
-        pieces = [
-            gathered_sum(cs, inner + inner * matrix + SHARE * chunk, SHARE)
-            for chunk in range(inner // SHARE)
-        ]
-        share = jnp.concatenate(pieces, axis=1)
+        share = joined_sum(cs, inner + inner * matrix, inner // SHARE)
         part_ref[matrix] = share
-        left_ref[:, at : at + inner] = exact(
-            start_ref[3 + matrix], share + attn_err[3 + matrix], TN
-        )
+        merged = share + attn_err[3 + matrix]
+        part_sum[matrix] = merged
+        left_ref[:, at : at + inner] = project(start_ref[3 + matrix], merged, NN)
         at += inner
     for matrix in range(2):
-        share = gathered_sum(cs, 0, inner) if matrix == 0 else gathered_sum(fs, 3 * units, inner)
+        share = gathered_sum(cs, 0, inner) if matrix == 0 else relayed_sum(fs, 3 * units, inner)
         out_grad[matrix] = share
-        left_ref[:, at : at + inner] = exact(
-            start_ref[6 + matrix], share + out_err[matrix], (((0,), (1,)), ((), ()))
-        )
+        merged = share + out_err[matrix]
+        out_sum[matrix] = merged
+        left_ref[:, at : at + inner] = project(start_ref[6 + matrix], merged, NT)
         at += inner
     for matrix in range(2):
-        pieces = [
-            gathered_sum(fs, units * matrix + SHARE * chunk, SHARE)
-            for chunk in range(units // SHARE)
-        ]
-        share = jnp.concatenate(pieces, axis=1)
+        share = joined_sum(fs, units * matrix, units // SHARE)
         ffin_grad[matrix] = share
-        left_ref[:, at : at + units] = exact(
-            start_ref[8 + matrix], share + ffin_err[matrix], TN
-        )
+        merged = share + ffin_err[matrix]
+        ffin_sum[matrix] = merged
+        left_ref[:, at : at + units] = project(start_ref[8 + matrix], merged, NN)
         at += units
-    share = gathered_sum(fs, 2 * units, units)
+    share = relayed_sum(fs, 2 * units, units)
     ffout_grad[...] = share
-    left_ref[:, at : at + units] = exact(
-        start_ref[10], share + ffout_err[...], (((0,), (1,)), ((), ()))
-    )
+    merged = share + ffout_err[...]
+    ffout_sum[...] = merged
+    left_ref[:, at : at + units] = project(start_ref[10], merged, NT)
 
 
 def tail_first(fs, cs, errors, start):
     inner = H * DK
     units = errors[3].shape[0]
+    shapes = [
+        shape_of((3, SHARE, inner), f32),
+        shape_of((2, inner, SHARE), f32),
+        shape_of((2, SHARE, units), f32),
+        shape_of((units, SHARE), f32),
+    ]
     return pl.pallas_call(
         tail_kernel,
-        out_shape=[
-            shape_of((3, SHARE, inner), f32),
-            shape_of((2, inner, SHARE), f32),
-            shape_of((2, SHARE, units), f32),
-            shape_of((units, SHARE), f32),
-            shape_of((8, 5 * inner + 3 * units), f32),
-        ],
+        out_shape=shapes * 2 + [shape_of((8, 5 * inner + 3 * units), f32)],
         name="tail_first",
     )(*fs, *cs, *errors, start)
 
 
 def tail_qkv_kernel(*refs):
-    qs, ts = refs[0:4], refs[4:8]
-    attn_err, start_ref, part_ref, grad_ref, left_ref = refs[8:]
+    qs = refs[0:4]
+    attn_err, start_ref, part_ref, part_sum, grad_ref, sum_ref, left_ref = refs[4:]
     inner = H * DK
     for matrix in range(3):
-        pieces = [
-            gathered_sum(qs, inner * matrix + SHARE * chunk, SHARE)
-            for chunk in range(inner // SHARE)
-        ]
-        share = jnp.concatenate(pieces, axis=1)
+        share = joined_sum(qs, inner * matrix, inner // SHARE)
         grad_ref[matrix] = share
         grad_ref[3 + matrix] = part_ref[matrix]
-        left_ref[:, inner * matrix : inner * (matrix + 1)] = exact(
-            start_ref[matrix], share + attn_err[matrix], TN
+        merged = share + attn_err[matrix]
+        sum_ref[matrix] = merged
+        sum_ref[3 + matrix] = part_sum[matrix]
+        left_ref[:, inner * matrix : inner * (matrix + 1)] = project(
+            start_ref[matrix], merged, NN
         )
-    small = gathered_sum(ts, 0, 32)
-    base = 3 * inner
-    left_ref[:, base : base + SHARE] = small[0:8]
-    left_ref[:, base + SHARE : base + 2 * SHARE] = small[8:16]
-    left_ref[:, base + 2 * SHARE :] = small[16:24] + small[24:32]
-
-
-def tail_qkv(qs, ts, attn_err, start, part):
-    inner = H * DK
+
+
+def tail_qkv(qs, attn_err, start, part, part_sum):
     return pl.pallas_call(
         tail_qkv_kernel,
         out_shape=[
             shape_of(attn_err.shape, f32),
-            shape_of((8, 3 * inner + 3 * SHARE), f32),
+            shape_of(attn_err.shape, f32),
+            shape_of((8, 3 * H * DK), f32),
         ],
         name="tail_qkv",
-    )(*qs, *ts, attn_err, start, part)
+    )(*qs, attn_err, start, part, part_sum)
 
 
 def orthonormal(current):
@@ -968,60 +1044,122 @@
     return slice(None) if group == 3 else at
 
 
-def right_kernel(replicas, listed, groups, total_ref, *refs):
+def owned_row(here_ref, rows, per):
+    return pltpu.roll(rows, lax.rem(SHARE - per * here_ref[0], SHARE), 1)[:, :per]
+
+
+def owned_bias(here_ref, tile, per):
+    turned_tile = pltpu.roll(tile, lax.rem(SHARE - per * here_ref[0], SHARE), 1).T
+    return turned_tile[:per, :H]
+
+
+def right_kernel(replicas, listed, groups, per, here_ref, total_ref, *refs):
     count = len(groups)
-    grads = dict(zip(groups, refs[:count]))
-    errors = dict(zip(groups, refs[count : 2 * count]))
-    left_ref, right_ref = refs[2 * count :]
+    merged = dict(zip(groups, refs[:count]))
+    if per:
+        ts = refs[count : count + 4]
+        left_ref, right_ref, gains_ref, bias_ref = refs[count + 4 :]
+        small = gathered_sum(ts, 0, 32)
+        base = 8 * len(listed)
+        right_ref[base : base + 16, :] = small[:16]
+        right_ref[base + 16 :, :] = small[16:24] + small[24:]
+        for row in range(3):
+            gains_ref[row] = small[row : row + 1]
+        for head in range(H):
+            bias_ref[head] = owned_row(here_ref, small[8 + head : 9 + head], per)
+    else:
+        left_ref, right_ref = refs[count:]
+    lefts = [
+        orthonormal(
+            total_ref[:, base - listed[0][2] : base - listed[0][2] + width] * (1.0 / replicas)
+        )
+        for group, at, base, width in listed
+    ]
     for index, (group, at, base, width) in enumerate(listed):
-        columns = slice(base - listed[0][2], base - listed[0][2] + width)
-        left = orthonormal(total_ref[:, columns] * (1.0 / replicas))
-        left_ref[:, columns] = left
-        spot = spot_of(group, at)
-        merged = grads[group][spot] + errors[group][spot]
-        right_ref[8 * index : 8 * (index + 1), :] = exact(
-            left, merged, NN if group in (1, 3) else NT
+        left_ref[:, base - listed[0][2] : base - listed[0][2] + width] = lefts[index]
+        right_ref[8 * index : 8 * (index + 1), :] = project(
+            lefts[index], merged[group][spot_of(group, at)], NN if group in (1, 3) else NT
         )
 
 
-def tail_right(replicas, listed, total, grads, errors):
+def in_vmem(values):
+    return [pl.BlockSpec(memory_space=pltpu.VMEM)] * len(values)
+
+
+def tail_right(replicas, listed, here, total, merged, ts=(), per=0):
     groups = tuple(sorted(set(item[0] for item in listed)))
     lanes = sum(item[3] for item in listed)
+    inputs = [total] + [merged[group] for group in groups] + list(ts)
+    shapes = [
+        shape_of((8, lanes), f32),
+        shape_of((8 * len(listed) + (24 if per else 0), SHARE), f32),
+    ]
+    if per:
+        shapes += [shape_of((3, 1, SHARE), f32), shape_of((H, 1, per), f32)]
     return pl.pallas_call(
-        functools.partial(right_kernel, replicas, listed, groups),
-        out_shape=[shape_of((8, lanes), f32), shape_of((8 * len(listed), SHARE), f32)],
+        functools.partial(right_kernel, replicas, listed, groups, per),
+        in_specs=[scalars()] + in_vmem(inputs),
+        out_shape=shapes,
         name="tail_right",
-    )(total, *[grads[group] for group in groups], *[errors[group] for group in groups])
-
-
-def final_kernel(replicas, listed, groups, more, *refs):
+    )(here, *inputs)
+
+
+def final_kernel(replicas, listed, groups, more, per, here_ref, *refs):
     rights, lefts, refs = refs[0:more], refs[more : 2 * more], refs[2 * more :]
     count = len(groups)
-    grads, errors, moments, new_errors, new_moments, updates = (
-        dict(zip(groups, refs[count * at : count * (at + 1)])) for at in range(6)
-    )
-    factor_ref = refs[6 * count]
+    merged, moments, new_errors, new_moments, updates = (
+        {} for _ in range(5)
+    )
+    for at, table in enumerate((merged, moments)):
+        table.update(zip(groups, refs[count * at : count * (at + 1)]))
+    refs = refs[2 * count :]
+    if per:
+        gain_moment, bias_moment, late_factors = refs[0:3]
+        refs = refs[3:]
+    for at, table in enumerate((new_errors, new_moments, updates)):
+        table.update(zip(groups, refs[count * at : count * (at + 1)]))
+    factor_ref = refs[3 * count]
     for place, (source, row, base, group, at, width) in enumerate(listed):
         mean = rights[source][8 * row : 8 * (row + 1), :] * (1.0 / replicas)
-        factor_ref[place] = mean.T
+        factor_ref[place] = mean
         left = lefts[source][:, base : base + width]
-        change = exact(left, mean, TN) if group in (1, 3) else exact(mean, left, TN)
+        change = outer_product(left, mean) if group in (1, 3) else outer_product(mean, left)
         spot = spot_of(group, at)
-        new_errors[group][spot] = grads[group][spot] + errors[group][spot] - change
+        new_errors[group][spot] = merged[group][spot] - change
         moment = decay * moments[group][spot] + change
         new_moments[group][spot] = moment
         updates[group][spot] = -rates[group] * moment
-
-
-def tail_final(replicas, listed, rights, lefts, grads, errors, moments):
+    if per:
+        factor_ref[len(listed) :] = late_factors[...]
+        new_gain, new_bias, gain_update, bias_update, rms_ref = refs[3 * count + 1 :]
+        base = rights[0].shape[0] - 24
+        moment = decay * gain_moment[...] + rights[0][base : base + 3, :] * (1.0 / replicas)
+        new_gain[...] = moment
+        gain_update[...] = -rates[4] * moment
+        mean = owned_bias(here_ref, rights[0][base + 8 : base + 16, :], per) * (1.0 / replicas)
+        moment = decay * bias_moment[...] + mean
+        new_bias[...] = moment
+        bias_update[...] = -rates[5] * moment
+        totals = jnp.sum(rights[0][base + 16 :, :].T, axis=0, keepdims=True)
+        rms_ref[...] = jnp.sqrt(totals[:, 0:4] / totals[:, 4:5])
+
+
+def tail_final(replicas, listed, here, rights, lefts, merged, moments, extra=(), per=0):
     groups = tuple(sorted(set(item[3] for item in listed)))
-    picked = [table[group] for table in (grads, errors, moments) for group in groups]
+    picked = [table[group] for table in (merged, moments) for group in groups]
     shapes = [shape_of(moments[group].shape, f32) for group in groups]
+    inputs = [*rights, *lefts, *picked, *extra]
+    small = [shape_of(value.shape, f32) for value in extra[:2]] * 2
+    factors = len(listed)
+    if per:
+        small.append(shape_of((1, 4), f32))
+        factors += extra[2].shape[0]
     return pl.pallas_call(
-        functools.partial(final_kernel, replicas, listed, groups, len(rights)),
-        out_shape=shapes * 3 + [shape_of((len(listed), SHARE, 8), f32)],
+        functools.partial(final_kernel, replicas, listed, groups, len(rights), per),
+        in_specs=[scalars()] + in_vmem(inputs),
+        out_shape=shapes * 3 + [shape_of((factors, 8, SHARE), f32)] + small,
         name="tail_final",
-    )(*rights, *lefts, *picked)
+    )(here, *inputs)
 
 
 def swap(value, axis, bit):
@@ -1029,19 +1167,23 @@
     return lax.ppermute(value, axis, [(at, at ^ bit) for at in range(size)])
 
 
-def sum_over(value, axis):
-    bit = 1
+def sum_over(value, axis, bit=1):
     while bit < lax.axis_size(axis):
         value = value + swap(value, axis, bit)
         bit *= 2
     return value
 
 
+def joined_half(kept, received):
+    total = kept.astype(f32) + received[kept.shape[0] :].astype(f32)
+    return total.astype(bf16)
+
+
 def after(value, *others):
     return lax.optimization_barrier((value,) + others)[0]
 
 
-def body(
+def layer(
     block_input,
     cotangent,
     encoder_states,
@@ -1065,7 +1207,7 @@
     err_ff_out,
     q_start,
 ):
-    length, width = block_input.shape[1:]
+    _, width = block_input.shape[1:]
     replicas = lax.axis_size("rep")
     owners = lax.axis_size("grp")
     buckets = rel_bias.shape[0] * owners
@@ -1074,7 +1216,6 @@
     stream = block_input[0]
     states = encoder_states[0]
     segment = segment_ids[0]
-    valid = (segment > 0).astype(f32)[:, None]
 
     small = jnp.concatenate(
         [norm_gains, jnp.pad(rel_bias, ((0, 0), (0, SHARE - H))), jnp.zeros((5, SHARE), f32)],
@@ -1087,9 +1228,9 @@
     )
     gains = ordered[:, 0:3].transpose(1, 0, 2).reshape(3, width).astype(f32)
     table_low = ordered[:, 3:11, :H].reshape(buckets, H)
-    first = w_attn[0:3].astype(bf16)
+    first = low_first(w_attn)
     first_shares = [first] + [
-        swap(after(first, smalls[-1]), "grp", step) for step in range(1, owners)
+        swap(after(first, *smalls[1:]), "grp", step) for step in range(1, owners)
     ]
     one, two, one_half, two_half = pack_weights(here, w_attn, w_attn_out, w_ff_in, w_ff_out)
     bias = bias_tiles(bucket_table, table_low)
@@ -1101,20 +1242,21 @@
     one_mine = [swap(one_half, "grp", step) for step in range(1, owners)]
 
     heads, normed0, qkv_full = qkv_forward(here, stream, gains, first_shares)
+    heads, two_half = lax.optimization_barrier((heads, two_half))
+    two_mine = [swap(two_half, "grp", step) for step in range(1, owners)]
     attended, self_logs = self_forward(heads, bias, kseg, qseg)
-    attended, two_half, *one_mine = lax.optimization_barrier((attended, two_half, *one_mine))
+    attended, *one_mine = lax.optimization_barrier((attended, *one_mine))
     one_other = [swap(part, "rep", 1) for part in one_mine]
-    two_mine = [swap(two_half, "grp", step) for step in range(1, owners)]
     hidden1, normed1, cross_query, cross_pairs, sums1, wo_full, co_full, cross_full = middle_forward(
-        here, attended, stream, valid, states, gains, one, one_mine, one_other
-    )
+        here, attended, stream, kseg, states, gains, one, one_mine, one_other
+    )
+    cross_query, *two_mine = lax.optimization_barrier((cross_query, *two_mine))
+    two_other = [swap(part, "rep", 1) for part in two_mine]
     cross_attended, cross_logs = cross_forward(cross_query, cross_pairs)
-    cross_attended, *two_mine = lax.optimization_barrier((cross_attended, *two_mine))
-    two_other = [swap(part, "rep", 1) for part in two_mine]
-    (block_output, grad_h2, grad_cross_att, sums2, gain2, f_own, *f_sends) = outer_layer(
-        here, cross_attended, hidden1, valid, cotangent[0], gains, co_full, two, two_mine, two_other
-    )
-    f_parts = [swap(part, "grp", step) for step, part in zip(range(1, owners), f_sends)]
+    (block_output, grad_h2, grad_cross_att, sums2, gain2, f_own, to_x, to_y, keep_y, keep_x) = outer_layer(
+        here, cross_attended, hidden1, kseg, cotangent[0], gains, co_full, two, two_mine, two_other
+    )
+    from_x, from_y = swap(to_x, "grp", 1), swap(to_y, "grp", 2)
     grad_cross_query, grad_cross_pairs = cross_backward(
         cross_query, cross_pairs, grad_cross_att, cross_logs
     )
@@ -1122,65 +1264,70 @@
         here, grad_cross_query, hidden1, normed1, attended, grad_h2, grad_cross_pairs, states, gains,
         wo_full, cross_full,
     )
+    grad_attended, from_x, from_y = lax.optimization_barrier((grad_attended, from_x, from_y))
+    next_y = swap(joined_half(keep_y, from_x), "grp", 2)
+    next_x = swap(joined_half(keep_x, from_y), "grp", 1)
     c_parts = [swap(part, "grp", step) for step, part in zip(range(1, owners), c_sends)]
     head_grads, table_parts = self_backward(
         heads, grad_attended, self_logs, bias, kseg, qseg, bucket_table
     )
     q_own, *q_sends = qkv_weights(here, head_grads, normed0)
+    errors = (err_attn[0], err_attn_out[0], err_ff_in[0], err_ff_out[0])
+    moments = (mom_attn, mom_attn_out, mom_ff_in, mom_ff_out)
+    start = jnp.swapaxes(q_start, 1, 2)
+    head_grads, c_own, *q_sends = lax.optimization_barrier((head_grads, c_own, *q_sends))
     q_parts = [swap(part, "grp", step) for step, part in zip(range(1, owners), q_sends)]
+    *firsts, left_two = tail_first(
+        [f_own, from_x, next_y, from_y, next_x], [c_own] + c_parts, errors, start
+    )
+    part, out_grad, ffin_grad, ffout_grad, part_sum, out_sum, ffin_sum, ffout_sum = firsts
+    left_two = left_two + swap(left_two, "rep", 1)
+    left_two, grad_h1 = lax.optimization_barrier((left_two, grad_h1))
     (input_grad, t_own, *t_sends) = last_backward(
         here, head_grads, stream, grad_h1, gains, qkv_full, table_parts, gain1, gain2, sums1, sums2
     )
     t_parts = [swap(part, "grp", step) for step, part in zip(range(1, owners), t_sends)]
-
-    errors = (err_attn[0], err_attn_out[0], err_ff_in[0], err_ff_out[0])
-    moments = (mom_attn, mom_attn_out, mom_ff_in, mom_ff_out)
-    part, out_grad, ffin_grad, ffout_grad, left_two = tail_first(
-        [f_own] + f_parts, [c_own] + c_parts, errors, q_start
-    )
-    left_two = sum_over(left_two, "rep")
-    attn_grad, left_one = tail_qkv(
-        [q_own] + q_parts, [t_own] + t_parts, errors[0], q_start, part
-    )
+    left_two = left_two + swap(left_two, "rep", 2)
+    left_two = sum_over(left_two, "rep", 4)
+    attn_grad, attn_sum, left_one = tail_qkv(
+        [q_own] + q_parts, errors[0], start, part, part_sum
+    )
+    left_one = left_one + swap(left_one, "rep", 1)
+    left_one, left_two = lax.optimization_barrier((left_one, left_two))
+    listed = matrices(H * DK, w_ff_out.shape[0])
     base = 3 * H * DK
-    share_gains = left_one[0:3, base : base + SHARE]
-    table_sum = left_one[0:H, base + SHARE : base + SHARE + buckets]
-    share_bias = lax.dynamic_slice_in_dim(
-        table_sum, group * (buckets // owners), buckets // owners, 1
-    ).T
-    left_one = sum_over(left_one, "rep")
-    mean_gains = left_one[0:3, base : base + SHARE] / replicas
-    mean_bias = lax.dynamic_slice_in_dim(
-        left_one[0:H, base + SHARE : base + SHARE + buckets] / replicas,
-        group * (buckets // owners), buckets // owners, 1,
-    ).T
-    totals = jnp.sum(left_one[0:5, base + 2 * SHARE :], axis=1)
-    branch_rms = jnp.sqrt(totals[0:4] / totals[4])
-    listed = matrices(H * DK, w_ff_out.shape[0])
-    later = (part, out_grad, ffin_grad, ffout_grad)
-    late_list = [(group, at - 3 if group == 0 else at, at_lane, lanes)
-                 for group, at, at_lane, lanes in listed[3:]]
-    late_errors = (err_attn[0, 3:], *errors[1:])
-    left_late, right_late = tail_right(replicas, late_list, left_two, later, late_errors)
+    per = buckets // owners
+    late_list = [(group, at - 3 if group == 0 else at, lane, lanes)
+                 for group, at, lane, lanes in listed[3:]]
+    left_late, right_late = tail_right(
+        replicas, late_list, here, left_two, (part_sum, out_sum, ffin_sum, ffout_sum)
+    )
+    left_one = sum_over(left_one, "rep", 2)
+    sums = (attn_sum, out_sum, ffin_sum, ffout_sum)
     right_late = sum_over(right_late, "rep")
-    grads = (attn_grad, out_grad, ffin_grad, ffout_grad)
+    left_early, right_early, share_gains, share_bias = tail_right(
+        replicas, listed[:3], here, left_one, sums, [t_own] + t_parts, per
+    )
+    right_early = right_early + swap(right_early, "rep", 1)
+    right_early, right_late = lax.optimization_barrier((right_early, right_late))
     finals_late = tail_final(
         replicas,
         [(0, 3 + place, item[2] - base, item[0], item[1], item[3])
          for place, item in enumerate(listed[6:])],
-        [right_late], [left_late], grads, errors, moments,
-    )
-    left_early, right_early = tail_right(replicas, listed[:3], left_one, grads, errors)
-    right_early = sum_over(right_early, "rep")
+        here, [right_late], [left_late], sums, moments,
+    )
+    right_early = sum_over(right_early, "rep", 2)
     finals = tail_final(
         replicas,
         [(0, place, item[2], item[0], item[1], item[3]) for place, item in enumerate(listed[:3])]
         + [(1, place, item[2] - base, item[0], item[1], item[3])
            for place, item in enumerate(listed[3:6])],
-        [right_early, right_late], [left_early, left_late], grads, errors, moments,
-    )
-    gain_moment = decay * mom_gains + mean_gains
-    bias_moment = decay * mom_bias + mean_bias
+        here, [right_early, right_late], [left_early, left_late], sums, moments,
+        (mom_gains, mom_bias, finals_late[9]), per,
+    )
+    gain_moment, bias_moment, gain_update, bias_update, branch_rms = finals[4:]
+    branch_rms = branch_rms[0]
+    factors = jnp.swapaxes(finals[3], 1, 2)
     return (
         block_output[None],
         input_grad[None],
@@ -1190,8 +1337,8 @@
         out_grad[None],
         ffin_grad[None],
         ffout_grad[None],
-        share_gains[None],
-        share_bias[None],
+        share_gains.transpose(1, 0, 2),
+        share_bias.transpose(1, 2, 0),
         finals[0][None],
         finals_late[0][None],
         finals_late[1][None],
@@ -1206,9 +1353,9 @@
         finals_late[6],
         finals_late[7],
         finals_late[8],
-        -rates[4] * gain_moment,
-        -rates[5] * bias_moment,
-        jnp.concatenate([finals[3], finals_late[9]], axis=0),
+        gain_update,
+        bias_update,
+        factors,
     )
 
 
@@ -1266,4 +1413,4 @@
         P("grp", None),
         P(None, "grp", None),
     )
-    return jax.shard_map(body, mesh=mesh, in_specs=in_specs, out_specs=out_specs, check_vma=False)
+    return jax.shard_map(layer, mesh=mesh, in_specs=in_specs, out_specs=out_specs, check_vma=False)

time: 289 us -> 236 us (0.82); the launches traced: 285 us -> 235 us
  Pallas kernels: 172 us -> 145 us
  waiting for transfers between devices: 37.3 us -> 28.7 us
  local copies, waits for them, and re-layouts: 13.3 us -> 5.71 us
  starting transfers between devices: 46.9 us -> 42.8 us
    ppermute x42 -> x43, waiting for transfers between devices: 37.3 us -> 28.7 us  [swap(): return lax.ppermute(value, axis, [(at, at ^ bit) for at in range(size)])]
    pallas_call x1, Pallas kernels: 14 us -> 7.56 us  [cross_forward(): pl.pallas_call(functools.partial(forward_kernel, False), grid=(pairs,), i...]
    pallas_call x8 -> x9, Pallas kernels: 55 us -> 49.5 us  [the longest x1 9.52 us: inner_backward(): call(inner_kernel, (steps,), [scalars(), rows_spec(TILE, inner), rows_spe...]
    pallas_call x1, Pallas kernels: 22.8 us -> 17.8 us  [self_backward(): pl.pallas_call(functools.partial(backward_kernel, True), grid=(pairs,), i...]
    pallas_call x1, Pallas kernels: 14.7 us -> 10.1 us  [self_forward(): pl.pallas_call(functools.partial(forward_kernel, True), grid=(pairs,), in...]
    ppermute x42 -> x43, starting transfers between devices: 46.9 us -> 42.8 us  [swap(): return lax.ppermute(value, axis, [(at, at ^ bit) for at in range(size)])]
    pallas_call x1, Pallas kernels: 14.1 us -> 11 us  [cross_backward(): pl.pallas_call(functools.partial(backward_kernel, False), grid=(pairs,),...]
    unnamed x80 -> x74, local copies, waits for them, and re-layouts: 5.93 us -> 4.16 us
  transfers between devices with their start and end apart: 42 -> 43, of which waited for: 12 -> 16; matrix products, arithmetic and copies ran while one was open for 7% -> 4% of each run, Pallas kernels for 47% -> 47%
where the time goes in v1:
time: 236 us; the launch traced here: 235 us
  Pallas kernels  145 us (61%)
  starting transfers between devices  42.8 us (18%)
  waiting for transfers between devices  28.7 us (12%)
  other arithmetic  11.9 us (5%)
  local copies, waits for them, and re-layouts  5.71 us (2%)
    ppermute x43, starting transfers between devices, swap(): return lax.ppermute(value, axis, [(at, at ^ bit) for at in range(size)])  42.8 us
    ppermute x43, waiting for transfers between devices, swap(): return lax.ppermute(value, axis, [(at, at ^ bit) for at in range(size)])  28.7 us
    pallas_call x1, Pallas kernels, outer_layer(): call(outer_kernel, (tokens // ROWS,), [scalars(), rows_spec(ROWS, inner),...  22.7 us
    pallas_call x1, Pallas kernels, self_backward(): pl.pallas_call(functools.partial(backward_kernel, True), grid=(pairs,), i...  17.8 us
    pallas_call x1, Pallas kernels, cross_backward(): pl.pallas_call(functools.partial(backward_kernel, False), grid=(pairs,),...  11 us
    pallas_call x1, Pallas kernels, self_forward(): pl.pallas_call(functools.partial(forward_kernel, True), grid=(pairs,), in...  10.1 us
    pallas_call x1, Pallas kernels, bias_tiles(): pl.pallas_call(functools.partial(bias_kernel, length), out_shape=jax.Shap...  9.91 us
    pallas_call x1, Pallas kernels, inner_backward(): call(inner_kernel, (steps,), [scalars(), rows_spec(TILE, inner), rows_spe...  9.52 us
  transfers between devices with their start and end apart: 43, of which 16 were waited for; matrix products, arithmetic and copies ran while one was open for 4% of the time, Pallas kernels for 47%

profile of v1, /device:TPU:0, one launch (start us, length us, event | category | flops | bytes accessed | tf_op | source)
XLA Modules:
  0.0 234.9 jit_solution(6467980934698108713)
XLA Ops:
  2.2 3.9 %collective-permute-start.2 = (bf16[16,128]{1,0:T(8,128)(2,1)S(1)}, bf16[16,128]{1,0:T(8,128)(2,1)S(1)}, u32[]{:S(2)}, u32[]{:S(2)}) collective-permute-start(bf16[16,128]{1,0:T(8,128)(2,1)S(1)} %maximum_maximum_fusion), channel_id=1, source_target_pairs={{0,24},{8,16},{16,8},{24,0},{1,25},{9,17},{17,9},{25,1},{2,26},{10... | collective-permute-start | bytes 12296 | tf_op jit(solution)/shard_map/ppermute | solution.py:1167
  13.0 3.2 %pack_weights.1 = (bf16[1920,128]{1,0:T(8,128)(2,1)}, bf16[3072,128]{1,0:T(8,128)(2,1)}, bf16[960,128]{1,0:T(8,128)(2,1)}, bf16[1536,128]{1,0:T(8,128)(2,1)}) custom-call(s32[2]{0:T(128)} %pad_add_fusion.here_ref, f32[6,128,384]{2,1,0:T(8,128)} %source_ref.1, f32[2,384,128]{2,1,0:T(8,128)} %out_ref.1, f32[2,128,1024]{2,1,0:T(8,128)} %ffin_ref.1, ...), custom_call_target="tpu_custom_call" | custom-call | tf_op jit(solution)/shard_map/pack_weights/pallas_call | solution.py:431
  16.3 2.9 %collective-permute-start.5 = (bf16[3,128,384]{2,1,0:T(8,128)(2,1)S(1)}, bf16[3,128,384]{2,1,0:T(8,128)(2,1)S(1)}, u32[]{:S(2)}, u32[]{:S(2)}) collective-permute-start(bf16[3,128,384]{2,1,0:T(8,128)(2,1)S(1)} %copy-done.2), channel_id=1, source_target_pairs={{0,24},{8,16},{16,8},{24,0},{1,25},{9,17},{17,9},{25,1},{2,26},{10... | collective-permute-start | bytes 884744 | tf_op jit(solution)/shard_map/ppermute | solution.py:1167
  20.5 9.9 %bias_tiles.1.refs_3_.refs_5_ = f32[6,1024,256]{2,1,0:T(8,128)} custom-call(s32[1,1024]{1,0:T(1,128)} %bitcast.55, bf16[32,6]{1,0:T(8,128)(2,1)} %fusion.3.table_ref), custom_call_target="tpu_custom_call" | custom-call | tf_op jit(solution)/shard_map/bias_tiles/pallas_call | solution.py:57
  37.0 5.3 %shard_map.422 = (bf16[3,1024,384]{2,1,0:T(8,128)(2,1)}, bf16[1024,512]{1,0:T(8,128)(2,1)}, bf16[512,1152]{1,0:T(8,128)(2,1)}) custom-call(s32[2]{0:T(128)} %pad_add_fusion.here_ref, bf16[1024,512]{1,0:T(8,128)(2,1)} %bitcast.40, f32[3,512]{1,0:T(4,128)} %convert_bitcast_fusion.gains_ref, bf16[3,128,384]{2,1,0:T(8,128)(2,1)} %shard_map.421.refs_0_, ...), custom_call_target="tpu_custom_call" | custom-call | tf_op jit(solution)/shard_map/pallas_call | solution.py:477
  42.3 10.1 %self_forward.1 = (bf16[1024,384]{1,0:T(8,128)(2,1)}, f32[3,8,1024]{2,1,0:T(8,128)}) custom-call(bf16[3,1024,384]{2,1,0:T(8,128)(2,1)} %get-tuple-element.153.refs_0_.refs_1_.refs_2_, bf16[3,1024,384]{2,1,0:T(8,128)(2,1)} %get-tuple-element.153.refs_0_.refs_1_.refs_2_, bf16[3,1024,384]{2,1,0:T(8,128)(2,1)} %get-tuple-element.153.refs_0_.refs_1_.refs_2_, ...), custom_call_target="tpu_custom_call" | custom-call | tf_op jit(solution)/shard_map/self_forward/pallas_call | solution.py:146
  58.7 6.9 %shard_map.423 = (f32[1024,512]{1,0:T(8,128)}, bf16[1024,512]{1,0:T(8,128)(2,1)}, bf16[1024,384]{1,0:T(8,128)(2,1)}, bf16[2,512,384]{2,1,0:T(8,128)(2,1)}, f32[8...) custom-call(s32[2]{0:T(128)} %pad_add_fusion.here_ref, ...), custom_call_target="tpu_custom_call" | custom-call | tf_op jit(solution)/shard_map/pallas_call | solution.py:547
  65.6 7.8 %collective-permute-done.13.m2 = bf16[1536,128]{1,0:T(8,128)(2,1)S(1)} collective-permute-done((bf16[1536,128]{1,0:T(8,128)(2,1)S(1)}, bf16[1536,128]{1,0:T(8,128)(2,1)S(1)}, u32[]{:S(2)}, u32[]{:S(2)}) %collective-permute-start.13) | collective-permute-done | bytes 393248 | tf_op jit(solution)/shard_map/ppermute | solution.py:1167
  74.1 7.6 %cross_forward.1 = (bf16[1024,384]{1,0:T(8,128)(2,1)}, f32[3,8,1024]{2,1,0:T(8,128)}) custom-call(bf16[1024,384]{1,0:T(8,128)(2,1)} %get-tuple-element.164.refs_0_, bf16[2,512,384]{2,1,0:T(8,128)(2,1)} %get-tuple-element.165.refs_1_.refs_2_, bf16[2,512,384]{2,1,0:T(8,128)(2,1)} %get-tuple-element.165.refs_1_.refs_2_), custom_call_target="tpu_custom_call" | custom-call | tf_op jit(solution)/shard_map/cross_forward/pallas_call | solution.py:170
  82.7 22.7 %shard_map.424 = (bf16[1024,512]{1,0:T(8,128)(2,1)}, f32[1024,512]{1,0:T(8,128)}, bf16[1024,384]{1,0:T(8,128)(2,1)}, f32[8,512]{1,0:T(8,128)}, f32[8,512]{1,0:T(...) custom-call(s32[2]{0:T(128)} %pad_add_fusion.here_ref, ...), custom_call_target="tpu_custom_call" | custom-call | tf_op jit(solution)/shard_map/pallas_call | solution.py:683
  107.6 11.0 %cross_backward.1 = (bf16[1024,384]{1,0:T(8,128)(2,1)}, bf16[2,512,384]{2,1,0:T(8,128)(2,1)}) custom-call(bf16[1024,384]{1,0:T(8,128)(2,1)} %get-tuple-element.164.refs_0_, bf16[2,512,384]{2,1,0:T(8,128)(2,1)} %get-tuple-element.165.refs_1_.refs_2_, bf16[2,512,384]{2,1,0:T(8,128)(2,1)} %get-tuple-element.165.refs_1_.refs_2_, ...), custom_call_target="tpu_custom_call" | custom-call | tf_op jit(solution)/shard_map/cross_backward/pallas_call | solution.py:326
  118.7 9.5 %shard_map.425 = (f32[1024,512]{1,0:T(8,128)}, bf16[1024,384]{1,0:T(8,128)(2,1)}, f32[512,512]{1,0:T(8,128)}, f32[8,512]{1,0:T(8,128)}, f32[1536,128]{1,0:T(8,12...) custom-call(s32[2]{0:T(128)} %pad_add_fusion.here_ref, ...), custom_call_target="tpu_custom_call" | custom-call | tf_op jit(solution)/shard_map/pallas_call | solution.py:768
  134.4 17.8 %self_backward.1 = (bf16[3,1024,384]{2,1,0:T(8,128)(2,1)}, f32[3,8,128]{2,1,0:T(8,128)}) custom-call(bf16[3,1024,384]{2,1,0:T(8,128)(2,1)} %get-tuple-element.153.refs_0_.refs_1_.refs_2_, bf16[3,1024,384]{2,1,0:T(8,128)(2,1)} %get-tuple-element.153.refs_0_.refs_1_.refs_2_, bf16[3,1024,384]{2,1,0:T(8,128)(2,1)} %get-tuple-element.153.refs_0_.refs_1_.refs_2_, ...), custom_call_target="tpu_custom_call" | custom-call | tf_op jit(solution)/shard_map/self_backward/pallas_call | solution.py:291
  152.2 4.9 %shard_map.426 = (f32[1152,128]{1,0:T(8,128)}, bf16[1152,128]{1,0:T(8,128)(2,1)}, bf16[1152,128]{1,0:T(8,128)(2,1)}, bf16[1152,128]{1,0:T(8,128)(2,1)}) custom-call(s32[2]{0:T(128)} %pad_add_fusion.here_ref, bf16[3,1024,384]{2,1,0:T(8,128)(2,1)} %get-tuple-element.193.heads_ref, bf16[1024,512]{1,0:T(8,128)(2,1)} %get-tuple-element.189.normed_ref), custom_call_target="tpu_custom_call" | custom-call | tf_op jit(solution)/shard_map/pallas_call | solution.py:824
  159.4 6.4 %tail_first.1 = (f32[3,128,384]{2,1,0:T(8,128)}, f32[2,384,128]{2,1,0:T(8,128)}, f32[2,128,1024]{2,1,0:T(8,128)}, f32[1024,128]{1,0:T(8,128)}, f32[3,128,384]{2,...) custom-call(f32[3456,128]{1,0:T(8,128)} %get-tuple-element.194.refs_0_, ...), custom_call_target="tpu_custom_call" | custom-call | tf_op jit(solution)/shard_map/tail_first/pallas_call | solution.py:987
  172.0 4.0 %collective-permute-done.30 = f32[8,4992]{1,0:T(8,128)S(1)} collective-permute-done((f32[8,4992]{1,0:T(8,128)S(1)}, f32[8,4992]{1,0:T(8,128)S(1)}, u32[]{:S(2)}, u32[]{:S(2)}) %collective-permute-start.30) | collective-permute-done | bytes 159776 | tf_op jit(solution)/shard_map/ppermute | solution.py:1167
  176.0 2.7 %collective-permute-start.31 = (f32[8,4992]{1,0:T(8,128)S(1)}, f32[8,4992]{1,0:T(8,128)S(1)}, u32[]{:S(2)}, u32[]{:S(2)}) collective-permute-start(f32[8,4992]{1,0:T(8,128)S(1)} %add.70), channel_id=1, source_target_pairs={{0,4},{1,5},{2,6},{3,7},{4,0},{5,1},{6,2},{7,3},{8,12},{9,13},{10,... | collective-permute-start | bytes 479240 | tf_op jit(solution)/shard_map/ppermute | solution.py:1167
  178.7 3.8 %collective-permute-done.27.refs_2_ = bf16[1152,128]{1,0:T(8,128)(2,1)S(1)} collective-permute-done((bf16[1152,128]{1,0:T(8,128)(2,1)S(1)}, bf16[1152,128]{1,0:T(8,128)(2,1)S(1)}, u32[]{:S(2)}, u32[]{:S(2)}) %collective-permute-start.27) | collective-permute-done | bytes 294944 | tf_op jit(solution)/shard_map/ppermute | solution.py:1167
  183.3 3.7 %tail_qkv.1 = (f32[6,128,384]{2,1,0:T(8,128)}, f32[6,128,384]{2,1,0:T(8,128)}, f32[8,1152]{1,0:T(8,128)}) custom-call(f32[1152,128]{1,0:T(8,128)} %get-tuple-element.214.refs_0_, bf16[1152,128]{1,0:T(8,128)(2,1)} %copy-done.19, bf16[1152,128]{1,0:T(8,128)(2,1)} %copy-done.20, bf16[1152,128]{1,0:T(8,128)(2,1)} %copy-done.21, f32[6,128,384]{2,1,0:T(8,128)} %bitcast.44, ...), custom_call_target="tpu_custom_call" | custom-call | tf_op jit(solution)/shard_map/tail_qkv/pallas_call | solution.py:1011
  191.4 4.6 %tail_right.3 = (f32[8,4992]{1,0:T(8,128)}, f32[64,128]{1,0:T(8,128)}) custom-call(s32[2]{0:T(128)} %pad_add_fusion.here_ref, f32[8,4992]{1,0:T(8,128)} %add.71.total_ref, f32[3,128,384]{2,1,0:T(8,128)} %get-tuple-element.219.refs_7_.refs_0_, f32[2,384,128]{2,1,0:T(8,128)} %get-tuple-element.230.refs_1_.refs_2_, ...), custom_call_target="tpu_custom_call" | custom-call | tf_op jit(solution)/shard_map/tail_right/pallas_call | solution.py:1099
  201.4 5.8 %shard_map.427 = (f32[1024,512]{1,0:T(8,128)}, f32[32,128]{1,0:T(8,128)}, bf16[32,128]{1,0:T(8,128)(2,1)}, bf16[32,128]{1,0:T(8,128)(2,1)}, bf16[32,128]{1,0:T(8,128)(2,1)}) custom-call(s32[2]{0:T(128)} %pad_add_fusion.here_ref, bf16[3,1024,384]{2,1,0:T(8,128)(2,1)} %get-tuple-element.193.heads_ref, bf16[1024,512]{1,0:T(8,128)(2,1)} %bitcast.42, ...), custom_call_target="tpu_custom_call" | custom-call | tf_op jit(solution)/shard_map/pallas_call | solution.py:873
  214.6 3.5 %tail_right.2 = (f32[8,1152]{1,0:T(8,128)}, f32[48,128]{1,0:T(8,128)}, f32[3,1,128]{2,1,0:T(1,128)}, f32[6,1,8]{2,1,0:T(1,128)}) custom-call(s32[2]{0:T(128)} %pad_add_fusion.here_ref, f32[8,1152]{1,0:T(8,128)} %add.73.total_ref, f32[6,128,384]{2,1,0:T(8,128)} %get-tuple-element.223.refs_0_.refs_4_, f32[32,128]{1,0:T(8,128)} %get-tuple-element.224.refs_1_, ...), custom_call_target="tpu_custom_call" | custom-call | tf_op jit(solution)/shard_map/tail_right/pallas_call | solution.py:1099
  225.1 5.0 %tail_final.2 = (f32[2,384,128]{2,1,0:T(8,128)}, f32[2,128,1024]{2,1,0:T(8,128)}, f32[1024,128]{1,0:T(8,128)}, f32[2,384,128]{2,1,0:T(8,128)}, f32[2,128,1024]{2...) custom-call(s32[2]{0:T(128)} %pad_add_fusion.here_ref, ...), custom_call_target="tpu_custom_call" | custom-call | tf_op jit(solution)/shard_map/tail_final/pallas_call | solution.py:1157
  230.7 4.0 %tail_final.3 = (f32[6,128,384]{2,1,0:T(8,128)}, f32[6,128,384]{2,1,0:T(8,128)}, f32[6,128,384]{2,1,0:T(8,128)}, f32[11,8,128]{2,1,0:T(8,128)}, f32[3,128]{1,0:T...) custom-call(s32[2]{0:T(128)} %pad_add_fusion.here_ref, f32[48,128]{1,0:T(8,128)} %add.79.refs_0_, ...), custom_call_target="tpu_custom_call" | custom-call | tf_op jit(solution)/shard_map/tail_final/pallas_call | solution.py:1157
  (186 shorter events, 66.7 us)
Async XLA Ops:
  2.2 14.1 %collective-permute-start.2 = (bf16[16,128]{1,0:T(8,128)(2,1)S(1)}, bf16[16,128]{1,0:T(8,128)(2,1)S(1)}, u32[]{:S(2)}, u32[]{:S(2)}) collective-permute-start(bf16[16,128]{1,0:T(8,128)(2,1)S(1)} %maximum_maximum_fusion), channel_id=1, source_target_pairs={{0,24},{8,16},{16,8},{24,0},{1,25},{9,17},{17,9},{25,1},{2,26},{10... | collective-permute-start | bytes 12296 | tf_op jit(solution)/shard_map/ppermute | solution.py:1167
  6.1 10.1 %collective-permute-start.1 = (bf16[16,128]{1,0:T(8,128)(2,1)S(1)}, bf16[16,128]{1,0:T(8,128)(2,1)S(1)}, u32[]{:S(2)}, u32[]{:S(2)}) collective-permute-start(bf16[16,128]{1,0:T(8,128)(2,1)S(1)} %maximum_maximum_fusion), channel_id=1, source_target_pairs={{0,16},{8,24},{16,0},{24,8},{1,17},{9,25},{17,1},{25,9},{2,18},{10... | collective-permute-start | bytes 12296 | tf_op jit(solution)/shard_map/ppermute | solution.py:1167
  16.3 14.2 %collective-permute-start.5 = (bf16[3,128,384]{2,1,0:T(8,128)(2,1)S(1)}, bf16[3,128,384]{2,1,0:T(8,128)(2,1)S(1)}, u32[]{:S(2)}, u32[]{:S(2)}) collective-permute-start(bf16[3,128,384]{2,1,0:T(8,128)(2,1)S(1)} %copy-done.2), channel_id=1, source_target_pairs={{0,24},{8,16},{16,8},{24,0},{1,25},{9,17},{17,9},{25,1},{2,26},{10... | collective-permute-start | bytes 884744 | tf_op jit(solution)/shard_map/ppermute | solution.py:1167
  19.2 12.6 %collective-permute-start.4 = (bf16[3,128,384]{2,1,0:T(8,128)(2,1)S(1)}, bf16[3,128,384]{2,1,0:T(8,128)(2,1)S(1)}, u32[]{:S(2)}, u32[]{:S(2)}) collective-permute-start(bf16[3,128,384]{2,1,0:T(8,128)(2,1)S(1)} %copy-done.2), channel_id=1, source_target_pairs={{0,16},{8,24},{16,0},{24,8},{1,17},{9,25},{17,1},{25,9},{2,18},{10... | collective-permute-start | bytes 884744 | tf_op jit(solution)/shard_map/ppermute | solution.py:1167
  19.7 12.3 %collective-permute-start.3 = (bf16[3,128,384]{2,1,0:T(8,128)(2,1)S(1)}, bf16[3,128,384]{2,1,0:T(8,128)(2,1)S(1)}, u32[]{:S(2)}, u32[]{:S(2)}) collective-permute-start(bf16[3,128,384]{2,1,0:T(8,128)(2,1)S(1)} %copy-done.2), channel_id=1, source_target_pairs={{0,8},{8,0},{16,24},{24,16},{1,9},{9,1},{17,25},{25,17},{2,10},{10... | collective-permute-start | bytes 884744 | tf_op jit(solution)/shard_map/ppermute | solution.py:1167
  32.0 20.4 %collective-permute-start.8 = (bf16[960,128]{1,0:T(8,128)(2,1)S(1)}, bf16[960,128]{1,0:T(8,128)(2,1)S(1)}, u32[]{:S(2)}, u32[]{:S(2)}) collective-permute-start(bf16[960,128]{1,0:T(8,128)(2,1)S(1)} %copy-done.36), channel_id=1, source_target_pairs={{0,24},{8,16},{16,8},{24,0},{1,25},{9,17},{17,9},{25,1},{2,26},{10... | collective-permute-start | bytes 737288 | tf_op jit(solution)/shard_map/ppermute | solution.py:1167
  33.6 18.9 %collective-permute-start.7 = (bf16[960,128]{1,0:T(8,128)(2,1)S(1)}, bf16[960,128]{1,0:T(8,128)(2,1)S(1)}, u32[]{:S(2)}, u32[]{:S(2)}) collective-permute-start(bf16[960,128]{1,0:T(8,128)(2,1)S(1)} %copy-done.36), channel_id=1, source_target_pairs={{0,16},{8,24},{16,0},{24,8},{1,17},{9,25},{17,1},{25,9},{2,18},{10... | collective-permute-start | bytes 737288 | tf_op jit(solution)/shard_map/ppermute | solution.py:1167
  34.9 17.5 %collective-permute-start.6 = (bf16[960,128]{1,0:T(8,128)(2,1)S(1)}, bf16[960,128]{1,0:T(8,128)(2,1)S(1)}, u32[]{:S(2)}, u32[]{:S(2)}) collective-permute-start(bf16[960,128]{1,0:T(8,128)(2,1)S(1)} %copy-done.36), channel_id=1, source_target_pairs={{0,8},{8,0},{16,24},{24,16},{1,9},{9,1},{17,25},{25,17},{2,10},{10... | collective-permute-start | bytes 737288 | tf_op jit(solution)/shard_map/ppermute | solution.py:1167
  52.6 13.0 %collective-permute-start.14 = (bf16[1536,128]{1,0:T(8,128)(2,1)S(1)}, bf16[1536,128]{1,0:T(8,128)(2,1)S(1)}, u32[]{:S(2)}, u32[]{:S(2)}) collective-permute-start(bf16[1536,128]{1,0:T(8,128)(2,1)S(1)} %copy-done.32), channel_id=1, source_target_pairs={{0,24},{8,16},{16,8},{24,0},{1,25},{9,17},{17,9},{25,1},{2,26},{10... | collective-permute-start | bytes 1179656 | tf_op jit(solution)/shard_map/ppermute | solution.py:1167
  54.2 19.2 %collective-permute-start.13 = (bf16[1536,128]{1,0:T(8,128)(2,1)S(1)}, bf16[1536,128]{1,0:T(8,128)(2,1)S(1)}, u32[]{:S(2)}, u32[]{:S(2)}) collective-permute-start(bf16[1536,128]{1,0:T(8,128)(2,1)S(1)} %copy-done.32), channel_id=1, source_target_pairs={{0,16},{8,24},{16,0},{24,8},{1,17},{9,25},{17,1},{25,9},{2,18},{10... | collective-permute-start | bytes 1179656 | tf_op jit(solution)/shard_map/ppermute | solution.py:1167
  55.6 17.9 %collective-permute-start.12 = (bf16[1536,128]{1,0:T(8,128)(2,1)S(1)}, bf16[1536,128]{1,0:T(8,128)(2,1)S(1)}, u32[]{:S(2)}, u32[]{:S(2)}) collective-permute-start(bf16[1536,128]{1,0:T(8,128)(2,1)S(1)} %copy-done.32), channel_id=1, source_target_pairs={{0,8},{8,0},{16,24},{24,16},{1,9},{9,1},{17,25},{25,17},{2,10},{10... | collective-permute-start | bytes 1179656 | tf_op jit(solution)/shard_map/ppermute | solution.py:1167
  105.4 23.0 %collective-permute-start.19 = (bf16[3584,128]{1,0:T(8,128)(2,1)}, bf16[3584,128]{1,0:T(8,128)(2,1)S(1)}, u32[]{:S(2)}, u32[]{:S(2)}) collective-permute-start(bf16[3584,128]{1,0:T(8,128)(2,1)} %get-tuple-element.184), channel_id=1, source_target_pairs={{0,16},{8,24},{16,0},{24,8},{1,17},{9,25},{17,1},{25,9},{2,18},{10... | collective-permute-start | bytes 2752520 | tf_op jit(solution)/shard_map/ppermute | solution.py:1167
  106.9 21.3 %collective-permute-start.18 = (bf16[3328,128]{1,0:T(8,128)(2,1)}, bf16[3328,128]{1,0:T(8,128)(2,1)S(1)}, u32[]{:S(2)}, u32[]{:S(2)}) collective-permute-start(bf16[3328,128]{1,0:T(8,128)(2,1)} %get-tuple-element.183), channel_id=1, source_target_pairs={{0,8},{8,0},{16,24},{24,16},{1,9},{9,1},{17,25},{25,17},{2,10},{10... | collective-permute-start | bytes 2555912 | tf_op jit(solution)/shard_map/ppermute | solution.py:1167
  128.5 29.9 %collective-permute-start.21 = (bf16[1792,128]{1,0:T(8,128)(2,1)S(1)}, bf16[1792,128]{1,0:T(8,128)(2,1)S(1)}, u32[]{:S(2)}, u32[]{:S(2)}) collective-permute-start(bf16[1792,128]{1,0:T(8,128)(2,1)S(1)} %add_convert_fusion), channel_id=1, source_target_pairs={{0,8},{8,0},{16,24},{24,16},{1,9},{9,1},{17,25},{25,17},{2,10},{10... | collective-permute-start | bytes 1376264 | tf_op jit(solution)/shard_map/ppermute | solution.py:1167
  130.2 28.2 %collective-permute-start.20 = (bf16[1664,128]{1,0:T(8,128)(2,1)S(1)}, bf16[1664,128]{1,0:T(8,128)(2,1)S(1)}, u32[]{:S(2)}, u32[]{:S(2)}) collective-permute-start(bf16[1664,128]{1,0:T(8,128)(2,1)S(1)} %add_convert_fusion.1), channel_id=1, source_target_pairs={{0,16},{8,24},{16,0},{24,8},{1,17},{9,25},{17,1},{25,9},{2,18},{10... | collective-permute-start | bytes 1277960 | tf_op jit(solution)/shard_map/ppermute | solution.py:1167
  131.0 26.2 %collective-permute-start.22 = (bf16[1536,128]{1,0:T(8,128)(2,1)}, bf16[1536,128]{1,0:T(8,128)(2,1)S(1)}, u32[]{:S(2)}, u32[]{:S(2)}) collective-permute-start(bf16[1536,128]{1,0:T(8,128)(2,1)} %get-tuple-element.200), channel_id=1, source_target_pairs={{0,8},{8,0},{16,24},{24,16},{1,9},{9,1},{17,25},{25,17},{2,10},{10... | collective-permute-start | bytes 1179656 | tf_op jit(solution)/shard_map/ppermute | solution.py:1167
  132.3 24.9 %collective-permute-start.23 = (bf16[1536,128]{1,0:T(8,128)(2,1)}, bf16[1536,128]{1,0:T(8,128)(2,1)S(1)}, u32[]{:S(2)}, u32[]{:S(2)}) collective-permute-start(bf16[1536,128]{1,0:T(8,128)(2,1)} %get-tuple-element.201), channel_id=1, source_target_pairs={{0,16},{8,24},{16,0},{24,8},{1,17},{9,25},{17,1},{25,9},{2,18},{10... | collective-permute-start | bytes 1179656 | tf_op jit(solution)/shard_map/ppermute | solution.py:1167
  132.9 25.4 %collective-permute-start.24 = (bf16[1536,128]{1,0:T(8,128)(2,1)}, bf16[1536,128]{1,0:T(8,128)(2,1)S(1)}, u32[]{:S(2)}, u32[]{:S(2)}) collective-permute-start(bf16[1536,128]{1,0:T(8,128)(2,1)} %get-tuple-element.202), channel_id=1, source_target_pairs={{0,24},{8,16},{16,8},{24,0},{1,25},{9,17},{17,9},{25,1},{2,26},{10... | collective-permute-start | bytes 1179656 | tf_op jit(solution)/shard_map/ppermute | solution.py:1167
  165.8 12.9 %collective-permute-start.26 = (bf16[1152,128]{1,0:T(8,128)(2,1)S(1)}, bf16[1152,128]{1,0:T(8,128)(2,1)S(1)}, u32[]{:S(2)}, u32[]{:S(2)}) collective-permute-start(bf16[1152,128]{1,0:T(8,128)(2,1)S(1)} %copy-done.35), channel_id=1, source_target_pairs={{0,8},{8,0},{16,24},{24,16},{1,9},{9,1},{17,25},{25,17},{2,10},{10... | collective-permute-start | bytes 884744 | tf_op jit(solution)/shard_map/ppermute | solution.py:1167
  167.1 15.4 %collective-permute-start.27 = (bf16[1152,128]{1,0:T(8,128)(2,1)S(1)}, bf16[1152,128]{1,0:T(8,128)(2,1)S(1)}, u32[]{:S(2)}, u32[]{:S(2)}) collective-permute-start(bf16[1152,128]{1,0:T(8,128)(2,1)S(1)} %copy-done.34), channel_id=1, source_target_pairs={{0,16},{8,24},{16,0},{24,8},{1,17},{9,25},{17,1},{25,9},{2,18},{10... | collective-permute-start | bytes 884744 | tf_op jit(solution)/shard_map/ppermute | solution.py:1167
  167.9 14.5 %collective-permute-start.28 = (bf16[1152,128]{1,0:T(8,128)(2,1)S(1)}, bf16[1152,128]{1,0:T(8,128)(2,1)S(1)}, u32[]{:S(2)}, u32[]{:S(2)}) collective-permute-start(bf16[1152,128]{1,0:T(8,128)(2,1)S(1)} %copy-done.33), channel_id=1, source_target_pairs={{0,24},{8,16},{16,8},{24,0},{1,25},{9,17},{17,9},{25,1},{2,26},{10... | collective-permute-start | bytes 884744 | tf_op jit(solution)/shard_map/ppermute | solution.py:1167
  176.0 13.2 %collective-permute-start.31 = (f32[8,4992]{1,0:T(8,128)S(1)}, f32[8,4992]{1,0:T(8,128)S(1)}, u32[]{:S(2)}, u32[]{:S(2)}) collective-permute-start(f32[8,4992]{1,0:T(8,128)S(1)} %add.70), channel_id=1, source_target_pairs={{0,4},{1,5},{2,6},{3,7},{4,0},{5,1},{6,2},{7,3},{8,12},{9,13},{10,... | collective-permute-start | bytes 479240 | tf_op jit(solution)/shard_map/ppermute | solution.py:1167
  198.2 12.5 %collective-permute-start.39 = (f32[64,128]{1,0:T(8,128)S(1)}, f32[64,128]{1,0:T(8,128)S(1)}, u32[]{:S(2)}, u32[]{:S(2)}) collective-permute-start(f32[64,128]{1,0:T(8,128)S(1)} %add.75), channel_id=1, source_target_pairs={{0,2},{1,3},{2,0},{3,1},{4,6},{5,7},{6,4},{7,5},{8,10},{9,11},{10,... | collective-permute-start | bytes 98312 | tf_op jit(solution)/shard_map/ppermute | solution.py:1167
  198.7 12.4 %collective-permute-start.33 = (f32[8,1152]{1,0:T(8,128)S(1)}, f32[8,1152]{1,0:T(8,128)S(1)}, u32[]{:S(2)}, u32[]{:S(2)}) collective-permute-start(f32[8,1152]{1,0:T(8,128)S(1)} %add.72), channel_id=1, source_target_pairs={{0,4},{1,5},{2,6},{3,7},{4,0},{5,1},{6,2},{7,3},{8,12},{9,13},{10,... | collective-permute-start | bytes 110600 | tf_op jit(solution)/shard_map/ppermute | solution.py:1167
  (56 other events, 260.0 us)
